TPU v7x, 128 devices: a whole 4x4x4 slice. The times are simulated.
128 devices in a mesh: row: 16 (over y, x_hi, core), col: 8 (over z, x_lo).
Axes of the slice: x: 4 (x_hi: 2, x_lo: 2; x = x_hi * 2 + x_lo), y: 4, z: 4, core: 2. Of those that a mesh axis runs over, the one named last changes fastest.
Arguments:
- features: float32 [8192, 256], P('row', 'col'), may hold values from -6 to 6
- weight: float32 [256, 256], replicated, may hold values from -0.375 to 0.375
- layer_bias: float32 [256], P('col'), may hold values from -3 to 3
- out_weight: float32 [2, 256], P(None, 'col'), may hold values from -0.375 to 0.375
- adj_tiles: float32 [16, 8, 4, 128, 128], P('row', 'col'), may hold values from -0.5 to 0.5
- tile_rows: int32 [16, 8, 4], P('row', 'col'), may hold values from 0 to 3
- tile_cols: int32 [16, 8, 4], P('row', 'col'), may hold values from 0 to 63, as said below
- tile_count: int32 [16, 8], P('row', 'col'), may hold values from 0 to 4, as said below
- port_rows: int32 [16, 128], P('row'), may hold values from 0 to 511
- targets: float32 [2, 2048], P(None, 'row'), may hold values from -6 to 6
Outputs:
- hidden: float32 [8192, 256], P('row', 'col')
- predictions: float32 [2, 2048], P(None, 'row')
- grad_weight: float32 [256, 256], P(None, 'col')
- grad_bias: float32 [256], P('col')
- grad_out_weight: float32 [2, 256], P(None, 'col')
Inputs may be any that keep to these rules, and one draw needn't show every extreme that they name: tile_cols[r, c, k] >= 4 r + tile_rows[r, c, k]; the live slots of all devices name distinct tile positions. The live slots of a device are its first tile_count slots; some device has all 4 slots live.
All inputs are finite; a program needn't handle non-finite values.
Results may differ from a plain program's by a relative error of at most 0.00017.
Values sent between devices are 32-bit elements; how exact they have to be, the bound alone decides.
No kernel may reach another device: no remote copies, remote signals or barrier semaphores. Data moves between devices by JAX's collectives and lax.ppermute only.
A program may use at most 64 MiB of HBM per device.

v0:
```python
import jax
import jax.numpy as jnp
from jax import lax
from jax.sharding import PartitionSpec as P


def per_device(
    features,
    weight,
    layer_bias,
    out_weight,
    adj_tiles,
    tile_rows,
    tile_cols,
    tile_count,
    port_rows,
    targets,
):
    row_devices = lax.axis_size("row")
    tile_data = adj_tiles[0, 0]
    local_tiles = tile_rows[0, 0]
    col_tiles = tile_cols[0, 0]
    slot_total = tile_data.shape[0]
    tile_edge = tile_data.shape[1]
    local_rows = features.shape[0]
    row_tiles = local_rows // tile_edge
    all_tiles = row_tiles * row_devices
    live_mask = (jnp.arange(slot_total, dtype=jnp.int32) < tile_count[0, 0]).astype(jnp.float32)
    masked = tile_data * live_mask[:, None, None]
    global_tiles = lax.axis_index("row") * row_tiles + local_tiles
    tile_index = jnp.arange(all_tiles, dtype=jnp.int32)[:, None]
    place_rows = (tile_index == global_tiles[None, :]).astype(jnp.float32)
    place_cols = (tile_index == col_tiles[None, :]).astype(jnp.float32)

    def aggregate(rows_full):
        feat_width = rows_full.shape[1]
        everything = lax.all_gather(rows_full, "row", axis=0, tiled=True)
        blocks = everything.reshape(all_tiles, tile_edge, feat_width)
        own_blocks = rows_full.reshape(row_tiles, tile_edge, feat_width)
        direct = jnp.einsum(
            "kab,kbf->kaf", masked, blocks[col_tiles], precision=lax.Precision.HIGHEST
        )
        mirror = jnp.einsum(
            "kab,kaf->kbf", masked, own_blocks[local_tiles], precision=lax.Precision.HIGHEST
        )
        result = jnp.einsum("nk,kaf->naf", place_rows, direct, precision=lax.Precision.HIGHEST)
        result = result + jnp.einsum(
            "nk,kaf->naf", place_cols, mirror, precision=lax.Precision.HIGHEST
        )
        summed = lax.psum_scatter(
            result.reshape(lax.axis_size("row") * local_rows, feat_width),
            "row",
            scatter_dimension=0,
            tiled=True,
        )
        return lax.psum_scatter(summed, "col", scatter_dimension=1, tiled=True)

    x_full = lax.all_gather(features, "col", axis=1, tiled=True)
    z_rows = jnp.dot(x_full, weight, precision=lax.Precision.HIGHEST)
    pre = aggregate(z_rows) + layer_bias[None, :]
    sigma = jax.nn.sigmoid(pre)
    hidden = pre * sigma
    port_index = port_rows[0]
    port_hidden = hidden[port_index]
    partial_pred = jnp.einsum("of,pf->op", out_weight, port_hidden, precision=lax.Precision.HIGHEST)
    predictions = lax.psum(partial_pred, "col")
    errors = predictions - targets
    grad_out_part = jnp.einsum("op,pf->of", errors, port_hidden, precision=lax.Precision.HIGHEST)
    port_grad = jnp.einsum("op,of->pf", errors, out_weight, precision=lax.Precision.HIGHEST)
    grad_hidden = jnp.zeros_like(hidden).at[port_index].add(port_grad)
    grad_pre = grad_hidden * (sigma * (1.0 + pre * (1.0 - sigma)))
    grad_full = lax.all_gather(grad_pre, "col", axis=1, tiled=True)
    back = aggregate(grad_full)
    grad_weight_part = jnp.dot(x_full.T, back, precision=lax.Precision.HIGHEST)
    grad_bias_part = jnp.sum(grad_pre, axis=0)
    grad_weight, grad_bias, grad_out_weight = lax.psum(
        (grad_weight_part, grad_bias_part, grad_out_part), "row"
    )
    return (hidden, predictions, grad_weight, grad_bias, grad_out_weight)


def solution(mesh):
    placed = (
        P("row", "col"),
        P(),
        P("col"),
        P(None, "col"),
        P("row", "col", None, None, None),
        P("row", "col", None),
        P("row", "col", None),
        P("row", "col"),
        P("row", None),
        P(None, "row"),
    )
    return jax.shard_map(
        per_device,
        mesh=mesh,
        in_specs=placed,
        out_specs=(P("row", "col"), P(None, "row"), P(None, "col"), P("col"), P(None, "col")),
        check_vma=False,
    )
```

profile of v0, /device:TPU:0, one launch (start us, length us, event | category | flops | bytes accessed | tf_op | source)
XLA Modules:
  0.0 642.7 jit_solution(13437956215964822083)
XLA Ops:
  7.2 31.8 %all_gather.12 = f32[512,256]{0,1:T(8,128)S(1)} all-gather(f32[512,32]{0,1:T(8,128)} %param.10), channel_id=1, replica_groups=mesh['row'=16,'col'=8] {'col'}, dimensions={1}, use_global_device_ids=true | all-gather | bytes 589824 | tf_op jit(solution)/shard_map/all_gather | solution.py:58
  39.0 1.8 fusion.36
  42.2 1.6 gather_fusion.1
  45.2 1.7 fusion.9
  46.9 67.8 %all-gather.3.cloned.1.call-done = f32[8192,256]{1,0:T(8,128)} async-done(((f32[512,256]{1,0:T(8,128)}), f32[8192,256]{1,0:T(8,128)}) %all-gather.3.cloned.1.call-update) | async-done | bytes 8388624 | tf_op jit(solution)/shard_map/all_gather | solution.py:37
  114.6 4.0 gather_fusion
  120.2 3.6 fusion.4
  123.8 3.9 convolution_add_fusion.1
  127.7 8.3 %copy.34 = f32[64,128,256]{2,1,0:T(8,128)} copy(f32[64,128,256]{2,0,1:T(8,128)S(1)} %convolution_add_fusion.1) | data formatting | bytes 16777216 | tf_op jit(solution)/shard_map/add | solution.py:47
  136.1 100.2 %reduce-scatter.9.cloned.1.call-done = f32[512,256]{1,0:T(8,128)} async-done(((f32[8192,256]{1,0:T(8,128)}), f32[512,256]{1,0:T(8,128)}) %reduce-scatter.9.cloned.1.call-update) | async-done | bytes 524304 | tf_op jit(solution)/shard_map/reduce_scatter | solution.py:50
  236.3 2.0 copy.47
  238.5 37.5 %reduce-scatter.13.cloned.1.call-done = f32[32,512]{1,0:T(8,128)} async-done(((f32[256,512]{1,0:T(8,128)}), f32[32,512]{1,0:T(8,128)}) %reduce-scatter.13.cloned.1.call-update) | async-done | bytes 65552
  277.9 16.6 %psum.28 = f32[2,128]{1,0:T(2,128)S(1)} all-reduce(f32[2,128]{1,0:T(2,128)S(1)} %convolution_bitcast_fusion.1), channel_id=1, replica_groups=mesh['row'=16,'col'=8] {'col'}, use_global_device_ids=true, to_apply=%region_2.0 | all-reduce | flops 256 | bytes 2048 | tf_op jit(solution)/shard_map/psum | solution.py:66
  296.1 31.4 %all_gather.14 = f32[512,256]{0,1:T(8,128)} all-gather(f32[512,32]{0,1:T(8,128)S(1)} %copy.36), channel_id=1, replica_groups=mesh['row'=16,'col'=8] {'col'}, dimensions={1}, use_global_device_ids=true | all-gather | bytes 589824 | tf_op jit(solution)/shard_map/all_gather | solution.py:72
  330.1 69.6 %all-gather.5.cloned.1.call-done = f32[8192,256]{0,1:T(8,128)} async-done(((f32[512,256]{0,1:T(8,128)}), f32[8192,256]{0,1:T(8,128)}) %all-gather.5.cloned.1.call-update) | async-done | bytes 8388624 | tf_op jit(solution)/shard_map/all_gather | solution.py:37
  399.7 9.0 %copy.37 = f32[8192,256]{1,0:T(8,128)} copy(f32[8192,256]{0,1:T(8,128)} %all-gather.5.cloned.1.call-done) | data formatting | bytes 16777216 | tf_op jit(solution)/shard_map/all_gather | solution.py:37
  408.6 4.0 gather_fusion.3
  413.3 3.6 fusion.1
  416.8 3.9 convolution_add_fusion
  420.8 8.1 %copy.42 = f32[64,128,256]{2,1,0:T(8,128)} copy(f32[64,128,256]{2,0,1:T(8,128)S(1)} %convolution_add_fusion) | data formatting | bytes 16777216 | tf_op jit(solution)/shard_map/add | solution.py:47
  428.9 100.2 %reduce-scatter.11.cloned.1.call-done = f32[512,256]{1,0:T(8,128)} async-done(((f32[8192,256]{1,0:T(8,128)}), f32[512,256]{1,0:T(8,128)}) %reduce-scatter.11.cloned.1.call-update) | async-done | bytes 524304 | tf_op jit(solution)/shard_map/reduce_scatter | solution.py:50
  529.2 2.0 copy.49
  532.1 36.8 %reduce-scatter.15.cloned.1.call-done = f32[32,512]{1,0:T(8,128)} async-done(((f32[256,512]{1,0:T(8,128)}), f32[32,512]{1,0:T(8,128)}) %reduce-scatter.15.cloned.1.call-update) | async-done | bytes 65552
  570.3 65.6 %all-reduce = (f32[256,32]{0,1:T(8,128)}, f32[32]{0:T(128)}, f32[2,32]{1,0:T(2,128)}) all-reduce(f32[256,32]{0,1:T(8,128)S(1)} %convolution_bitcast_fusion, f32[32]{0:T(128)S(1)} %get-tuple-element.28, f32[2,32]{1,0:T(2,128)S(1)} %fusion.31), channel_id=1, replica_groups=mesh['row'=16,'col'=8] {'row'}, use_global_device_ids=true, to_apply=%region_6.0 | all-reduce | flops 8288 | bytes 66304 | tf_op jit(solution)/shard_map/psum | solution.py:76
  (54 shorter events, 12.9 us)
Async XLA Ops:
  7.2 31.8 %copy-start = (f32[256,256]{1,0:T(8,128)S(1)}, f32[256,256]{1,0:T(8,128)}, u32[]{:S(2)}) copy-start(f32[256,256]{1,0:T(8,128)} %param.11) | copy-start | bytes 786436
  7.2 116.6 %copy-start.6 = (s32[1,1,4]{2,1,0:T(1,128)S(1)}, s32[1,1,4]{2,1,0:T(1,128)}, u32[]{:S(2)}) copy-start(s32[1,1,4]{2,1,0:T(1,128)} %param.16) | copy-start | bytes 52
  7.2 107.5 %all-gather.3.cloned.1.call-start = ((), (), s32[]{:S(2)}) async-start(), calls=%async_computation.4 | async-start | bytes 8912896 | tf_op jit(solution)/shard_map/all_gather | solution.py:37
  40.9 195.5 %reduce-scatter.9.cloned.1.call-start = ((), (), s32[]{:S(2)}) async-start(), calls=%async_computation.5 | async-start | bytes 8912896 | tf_op jit(solution)/shard_map/reduce_scatter | solution.py:50
  136.0 102.4 %copy-start.8 = (s32[1,128]{1,0:T(1,128)S(1)}, s32[1,128]{1,0:T(1,128)}, u32[]{:S(2)}) copy-start(s32[1,128]{1,0:T(1,128)} %param.18) | copy-start | bytes 1540
  136.0 141.0 %copy-start.7 = (f32[32]{0:T(128)S(1)}, f32[32]{0:T(128)}, u32[]{:S(2)}) copy-start(f32[32]{0:T(128)} %param.12) | copy-start | bytes 388
  136.0 141.7 %copy-start.4 = (f32[2,32]{1,0:T(2,128)S(1)}, f32[2,32]{1,0:T(2,128)}, u32[]{:S(2)}) copy-start(f32[2,32]{1,0:T(2,128)} %param.13) | copy-start | bytes 772
  136.0 158.4 %copy-start.5 = (f32[2,128]{1,0:T(2,128)S(1)}, f32[2,128]{1,0:T(2,128)}, u32[]{:S(2)}) copy-start(f32[2,128]{1,0:T(2,128)} %param.19) | copy-start | bytes 3076
  136.0 193.3 %copy-start.2 = (f32[1,1,4,128,128]{4,3,2,1,0:T(8,128)S(1)}, f32[1,1,4,128,128]{4,3,2,1,0:T(8,128)}, u32[]{:S(2)}) copy-start(f32[1,1,4,128,128]{4,3,2,1,0:T(8,128)} %param.14) | copy-start | bytes 786436
  136.1 139.9 %reduce-scatter.13.cloned.1.call-start = ((), (), s32[]{:S(2)}) async-start(), calls=%async_computation.8 | async-start | bytes 589824
  238.4 161.3 %all-gather.5.cloned.1.call-start = ((), (), s32[]{:S(2)}) async-start(), calls=%async_computation.6 | async-start | bytes 8912896 | tf_op jit(solution)/shard_map/all_gather | solution.py:37
  294.4 237.5 %copy-start.3 = (f32[2,128]{1,0:T(2,128)}, f32[2,128]{1,0:T(2,128)S(1)}, u32[]{:S(2)}) copy-start(f32[2,128]{1,0:T(2,128)S(1)} %psum.28) | copy-start | bytes 3076
  327.4 201.7 %reduce-scatter.11.cloned.1.call-start = ((), (), s32[]{:S(2)}) async-start(), calls=%async_computation.7 | async-start | bytes 8912896 | tf_op jit(solution)/shard_map/reduce_scatter | solution.py:50
  420.8 215.1 %copy-start.1 = (f32[256,256]{1,0:T(8,128)S(1)}, f32[256,256]{1,0:T(8,128)}, u32[]{:S(2)}) copy-start(f32[256,256]{1,0:T(8,128)} %param.11) | copy-start | bytes 786436
  428.9 140.0 %reduce-scatter.15.cloned.1.call-start = ((), (), s32[]{:S(2)}) async-start(), calls=%async_computation.9 | async-start | bytes 589824
Sparse Core Ops, SparseCore 0:
  41.0 73.6 all-gather.2
  136.2 100.1 reduce-scatter.8
  238.7 37.2 reduce-scatter.12
  327.6 72.0 all-gather.4
  429.0 100.1 reduce-scatter.10
  531.5 37.3 reduce-scatter.14
where the time goes:
time: 643 us
  waiting for transfers between devices  412 us (64%)
  blocking collectives  145 us (23%)
  local copies, waits for them, and re-layouts  43.2 us (7%)
  matrix products  23.5 us (4%)
  between operations  15 us (2%)
    reduce_scatter x2, waiting for transfers between devices, aggregate(): lax.psum_scatter(result.reshape(lax.axis_size('row') * local_rows, feat_w...  200 us
    all_gather x2, waiting for transfers between devices, aggregate(): everything = lax.all_gather(rows_full, 'row', axis=0, tiled=True)  137 us
    unnamed x8, waiting for transfers between devices  74.4 us
    psum x1, blocking collectives, per_device(): lax.psum((grad_weight_part, grad_bias_part, grad_out_part), 'row')  65.6 us
    all_gather x1, blocking collectives, per_device(): x_full = lax.all_gather(features, 'col', axis=1, tiled=True)  31.8 us
    all_gather x1, blocking collectives, per_device(): grad_full = lax.all_gather(grad_pre, 'col', axis=1, tiled=True)  31.4 us
    psum x1, blocking collectives, per_device(): predictions = lax.psum(partial_pred, 'col')  16.6 us
    add x2, local copies, waits for them, and re-layouts, aggregate(): result + jnp.einsum('nk,kaf->naf', place_cols, mirror, precision=lax.Prec...  16.3 us
  transfers between devices with their start and end apart: 6, of which 6 were waited for; matrix products, arithmetic and copies ran while one was open for 1% of the time, Pallas kernels for 0%

commit v1 on v0

v1 whole, which is shorter than its diff:
```python
import functools

import jax
import jax.numpy as jnp
from jax import lax
from jax.experimental import pallas as pl
from jax.experimental.pallas import tpu as pltpu
from jax.sharding import PartitionSpec as P

F32 = jnp.float32
BF16 = jnp.bfloat16
VMEM = pl.BlockSpec(memory_space=pltpu.VMEM)
SMEM = pl.BlockSpec(memory_space=pltpu.SMEM)
NN = (((1,), (0,)), ((), ()))
NT = (((1,), (1,)), ((), ()))
TN = (((0,), (0,)), ((), ()))


def split(x):
    high = x.astype(BF16)
    low = (x - high.astype(F32)).astype(BF16)
    return high, low


def dot3(a, b, dims):
    ah, al = a
    bh, bl = b
    one = functools.partial(lax.dot_general, dimension_numbers=dims, preferred_element_type=F32)
    return one(ah, bh) + (one(al, bh) + one(ah, bl))


def stacked_dot3(a, b, dims):
    rows = a[0].shape[0]
    one = functools.partial(lax.dot_general, dimension_numbers=dims, preferred_element_type=F32)
    both = one(jnp.concatenate(a, axis=0), b[0])
    return both[:rows] + (both[rows:] + one(a[0], b[1]))


def pack_kernel(slots, rows_ref, cols_ref, count_ref, tiles_ref, side_ref, out_ref):
    edge = tiles_ref.shape[3]
    for k in range(slots):
        live = k < count_ref[0, 0]
        out_ref[0, k * edge : (k + 1) * edge, :] = jnp.where(live, tiles_ref[0, 0, k], 0.0)
    lane = lax.broadcasted_iota(jnp.int32, (1, edge), 1)
    meta = jnp.zeros((1, edge), jnp.int32)
    for k in range(slots):
        meta = jnp.where(lane == k, rows_ref[0, 0, k], meta)
        meta = jnp.where(lane == slots + k, cols_ref[0, 0, k], meta)
    out_ref[0, slots * edge : slots * edge + 8, :] = side_ref[...]
    out_ref[0, slots * edge : slots * edge + 1, :] = meta.astype(F32)


def mirror_kernel(slots, meta_ref, tiles_ref, x_ref, out_ref):
    edge = tiles_ref.shape[2]
    row_tiles = x_ref.shape[1] // edge
    out_ref[...] = jnp.zeros_like(out_ref)
    for d in range(tiles_ref.shape[0]):
        for k in range(slots):
            row = meta_ref[d, k]
            col = meta_ref[d, slots + k]
            x = split(x_ref[:, pl.ds(pl.multiple_of(row * edge, edge), edge)])
            u = split(tiles_ref[d, k * edge : (k + 1) * edge, :])
            lanes = pl.ds(pl.multiple_of((col % row_tiles) * edge, edge), edge)
            out_ref[col // row_tiles, :, lanes] += stacked_dot3(x, u, NN)


def direct_kernel(slots, meta_ref, tiles_ref, x_ref, part_ref, out_ref, total):
    edge = tiles_ref.shape[2]
    row_tiles = total.shape[1] // edge
    total[...] = jnp.sum(part_ref[...], axis=0)
    for d in range(tiles_ref.shape[0]):
        for k in range(slots):
            row = meta_ref[d, k]
            col = meta_ref[d, slots + k]
            lanes = pl.ds(pl.multiple_of((col % row_tiles) * edge, edge), edge)
            x = split(x_ref[col // row_tiles, :, lanes])
            u = split(tiles_ref[d, k * edge : (k + 1) * edge, :])
            here = pl.ds(pl.multiple_of(row * edge, edge), edge)
            total[:, here] += stacked_dot3(x, u, NT)
    for c in range(out_ref.shape[0]):
        out_ref[c] = total[...]


def main_kernel(
    y_ref, w_ref, side_ref, ports_ref, targets_ref, hidden_ref, pred_ref, grad_ref, wt, pre_p, hid_p, side_t
):
    me = lax.axis_index("col")
    cols, block, nodes = y_ref.shape
    feats = cols * block
    mine = pl.ds(pl.multiple_of(me * block, block), block)
    wt[...] = w_ref[...].T
    y = split(y_ref[...].reshape(feats, nodes))
    for c in range(cols):
        side_t[c * block : (c + 1) * block, :] = side_ref[c].T[:block, :]
    pre = stacked_dot3(split(wt[mine, :]), y, NN) + side_t[mine, 1:2]
    hidden_ref[...] = pre * jax.nn.sigmoid(pre)
    node = lax.broadcasted_iota(jnp.int32, (nodes, ports_ref.shape[1]), 0)
    pick = (node == ports_ref[...]).astype(BF16)
    one = functools.partial(lax.dot_general, dimension_numbers=NN, preferred_element_type=F32)
    yp = split(one(y[0], pick) + one(y[1], pick))
    pre_all = dot3(split(wt[...]), yp, NN) + side_t[:, 1:2]
    pre_p[...] = pre_all
    hid_all = pre_all * jax.nn.sigmoid(pre_all)
    hid_p[...] = hid_all
    weights = jnp.concatenate([side_ref[c, 2:4, :block] for c in range(cols)], axis=1)
    pred = dot3(split(weights), split(hid_all), NN)
    pred_ref[...] = pred
    err = pred - targets_ref[...]
    gow = dot3(split(err), split(hid_p[mine, :]), NT)
    pre_c = pre_p[mine, :]
    s = jax.nn.sigmoid(pre_c)
    port_grad = side_t[mine, 2:3] * err[0:1, :] + side_t[mine, 3:4] * err[1:2, :]
    grad_pre = port_grad * (s * (1.0 + pre_c * (1.0 - s)))
    gp = split(grad_pre)
    gw = stacked_dot3(gp, yp, NT)
    ones = jnp.ones((1, grad_pre.shape[1]), BF16)
    gb = lax.dot_general(ones, gp[0], NT, preferred_element_type=F32) + lax.dot_general(
        ones, gp[1], NT, preferred_element_type=F32
    )
    for r in range(grad_ref.shape[0]):
        grad_ref[r, :block, :] = gw
        grad_ref[r, block : block + 2, :block] = gow
        grad_ref[r, block + 2 : block + 3, :block] = gb


def final_kernel(parts_ref, gw_ref, gb_ref, gow_ref):
    block = gw_ref.shape[0]
    total = jnp.sum(parts_ref[...], axis=0)
    gw_ref[...] = total[:block, :]
    gow_ref[...] = total[block : block + 2, :block]
    gb_ref[...] = total[block + 2 : block + 3, :block]


def per_device(
    features,
    weight,
    layer_bias,
    out_weight,
    adj_tiles,
    tile_rows,
    tile_cols,
    tile_count,
    port_rows,
    targets,
):
    rows = lax.axis_size("row")
    cols = lax.axis_size("col")
    nodes, block = features.shape
    feats = weight.shape[0]
    slots, edge = adj_tiles.shape[2:4]
    outs = out_weight.shape[0]
    x_own = features.T
    x_all = lax.all_gather(x_own, "row", axis=0)

    side = jnp.zeros((8, edge), F32)
    side = side.at[1, :block].set(layer_bias).at[2 : 2 + outs, :block].set(out_weight)
    length = slots * edge + 8
    packed = pl.pallas_call(
        functools.partial(pack_kernel, slots),
        grid=(cols,),
        in_specs=[
            SMEM,
            SMEM,
            SMEM,
            pl.BlockSpec((1, 1, slots, edge, edge), lambda i: (0, 0, 0, 0, 0)),
            pl.BlockSpec((8, edge), lambda i: (0, 0)),
        ],
        out_specs=pl.BlockSpec((1, length, edge), lambda i: (i, 0, 0)),
        out_shape=jax.ShapeDtypeStruct((cols, length, edge), F32),
        name="pack",
    )(tile_rows, tile_cols, tile_count, adj_tiles, side)
    tiles = lax.all_to_all(packed, "col", 0, 0)
    meta = tiles[:, slots * edge, : 2 * slots].astype(jnp.int32)
    sides = tiles[:, slots * edge :, :]

    mirror = pl.pallas_call(
        functools.partial(mirror_kernel, slots),
        in_specs=[SMEM, VMEM, VMEM],
        out_specs=VMEM,
        out_shape=jax.ShapeDtypeStruct((rows, block, nodes), F32),
        name="mirror",
    )(meta, tiles, x_own)
    parts = lax.all_to_all(mirror, "row", 0, 0)
    y_own = pl.pallas_call(
        functools.partial(direct_kernel, slots),
        in_specs=[SMEM, VMEM, VMEM, VMEM],
        out_specs=VMEM,
        out_shape=jax.ShapeDtypeStruct((cols, block, nodes), F32),
        scratch_shapes=[pltpu.VMEM((block, nodes), F32)],
        name="direct",
    )(meta, tiles, x_all, parts)
    y = lax.all_to_all(y_own, "col", 0, 0)
    ports = port_rows.shape[1]
    hidden_t, predictions, grads = pl.pallas_call(
        main_kernel,
        in_specs=[VMEM] * 5,
        out_specs=[VMEM] * 3,
        out_shape=[
            jax.ShapeDtypeStruct((block, nodes), F32),
            jax.ShapeDtypeStruct((outs, ports), F32),
            jax.ShapeDtypeStruct((rows, block + 8, feats), F32),
        ],
        scratch_shapes=[
            pltpu.VMEM((feats, feats), F32),
            pltpu.VMEM((feats, ports), F32),
            pltpu.VMEM((feats, ports), F32),
            pltpu.VMEM((feats, 8), F32),
        ],
        name="main",
    )(y, weight, sides, port_rows, targets)
    all_grads = lax.all_to_all(grads, "row", 0, 0)
    gw, gb, gow = pl.pallas_call(
        final_kernel,
        in_specs=[VMEM],
        out_specs=[VMEM] * 3,
        out_shape=[
            jax.ShapeDtypeStruct((block, feats), F32),
            jax.ShapeDtypeStruct((1, block), F32),
            jax.ShapeDtypeStruct((outs, block), F32),
        ],
        name="final",
    )(all_grads)
    return (hidden_t.T, predictions, gw.T, gb[0], gow)


def solution(mesh):
    placed = (
        P("row", "col"),
        P(),
        P("col"),
        P(None, "col"),
        P("row", "col", None, None, None),
        P("row", "col", None),
        P("row", "col", None),
        P("row", "col"),
        P("row", None),
        P(None, "row"),
    )
    return jax.shard_map(
        per_device,
        mesh=mesh,
        in_specs=placed,
        out_specs=(P("row", "col"), P(None, "row"), P(None, "col"), P("col"), P(None, "col")),
        check_vma=False,
    )
```

time: 643 us -> 129 us (0.20)
  waiting for transfers between devices: 412 us -> 54.7 us
  blocking collectives: 145 us -> 18.1 us
  local copies, waits for them, and re-layouts: 43.2 us -> 6.61 us
  matrix products: 23.5 us -> 0 us
  Pallas kernels: 0 us -> 16.7 us
  starting transfers between devices: 0.25 us -> 16.6 us
    reduce_scatter x2 -> x0, waiting for transfers between devices: 200 us -> none  [aggregate(): lax.psum_scatter(result.reshape(lax.axis_size('row') * local_rows, feat_w...]
    all_gather x2 -> x1, waiting for transfers between devices: 137 us -> 12.1 us  [per_device(): x_all = lax.all_gather(x_own, 'row', axis=0)]
    psum x2 -> x0, blocking collectives: 82.1 us -> none  [the longest x1 65.6 us: per_device(): lax.psum((grad_weight_part, grad_bias_part, grad_out_part), 'row')]
    unnamed x8 -> x1, waiting for transfers between devices: 74.4 us -> 0.68 us
    all_gather x2 -> x0, blocking collectives: 63.1 us -> none  [the longest x1 31.8 us: per_device(): x_full = lax.all_gather(features, 'col', axis=1, tiled=True)]
    all_to_all x0 -> x3, waiting for transfers between devices: none -> 41.9 us  [the longest x1 27.3 us: per_device(): tiles = lax.all_to_all(packed, 'col', 0, 0)]
    dot_general x13 -> x0, matrix products: 23.5 us -> none  [the longest x2 7.9 us: aggregate(): jnp.einsum('nk,kaf->naf', place_cols, mirror, precision=lax.Precision.HIG...]
    all_to_all x0 -> x1, blocking collectives: none -> 18.1 us  [per_device(): all_grads = lax.all_to_all(grads, 'row', 0, 0)]
  transfers between devices with their start and end apart: 6 -> 4, of which waited for: 6 -> 4; matrix products, arithmetic and copies ran while one was open for 1% -> 2% of each run, Pallas kernels for 0% -> 3%
where the time goes in v1:
time: 129 us; the launch traced here: 128 us
  waiting for transfers between devices  54.7 us (42%)
  blocking collectives  18.1 us (14%)
  Pallas kernels  16.7 us (13%)
  starting transfers between devices  16.6 us (13%)
  between operations  14.7 us (11%)
  local copies, waits for them, and re-layouts  6.61 us (5%)
    all_to_all x1, waiting for transfers between devices, per_device(): tiles = lax.all_to_all(packed, 'col', 0, 0)  27.3 us
    all_to_all x1, blocking collectives, per_device(): all_grads = lax.all_to_all(grads, 'row', 0, 0)  18.1 us
    all_gather x1, waiting for transfers between devices, per_device(): x_all = lax.all_gather(x_own, 'row', axis=0)  12.1 us
    all_to_all x1, waiting for transfers between devices, per_device(): y = lax.all_to_all(y_own, 'col', 0, 0)  8.68 us
    all_to_all x1, starting transfers between devices, per_device(): parts = lax.all_to_all(mirror, 'row', 0, 0)  6.74 us
    all_to_all x1, starting transfers between devices, per_device(): tiles = lax.all_to_all(packed, 'col', 0, 0)  6.32 us
    all_to_all x1, waiting for transfers between devices, per_device(): parts = lax.all_to_all(mirror, 'row', 0, 0)  5.93 us
    pallas_call x1, Pallas kernels, per_device(): pl.pallas_call(functools.partial(direct_kernel, slots), in_specs=[SMEM, V...  4.43 us
  transfers between devices with their start and end apart: 4, of which 4 were waited for; matrix products, arithmetic and copies ran while one was open for 2% of the time, Pallas kernels for 3%

profile of v1, /device:TPU:0, one launch (start us, length us, event | category | flops | bytes accessed | tf_op | source)
XLA Modules:
  0.0 128.1 jit_solution(5115720233680113220)
XLA Ops:
  7.8 0.7 scatter.6
  8.5 1.5 %scatter.9.side_ref = f32[8,128]{1,0:T(8,128)S(1)} dynamic-update-slice(f32[8,128]{1,0:T(8,128)S(1)} %scatter.6, f32[2,32]{1,0:T(2,128)} %param.17, s32[]{:T(128)} %constant.56.clone.1, s32[]{:T(128)} %constant.57.clone.1) | dynamic-update-slice | bytes 516 | tf_op jit(solution)/shard_map/scatter | solution.py:156
  9.9 0.0 copy-start.3
  10.0 0.6 copy-done.3
  10.5 4.1 %pack.1 = f32[8,520,128]{2,1,0:T(8,128)} custom-call(s32[1,1,4]{2,1,0:T(1,128)} %rows_ref.1, s32[1,1,4]{2,1,0:T(1,128)} %cols_ref.1, s32[1,1]{1,0:T(1,128)S(6)} %copy.16.count_ref, f32[1,1,4,128,128]{4,3,2,1,0:T(8,128)} %tiles_ref.1, f32[8,128]{1,0:T(8,128)} %copy-done.3), custom_call_target="tpu_custom_call" | custom-call | tf_op jit(solution)/shard_map/pack/pallas_call | solution.py:158
  14.6 6.3 %all-to-all-start = ((f32[8,520,128]{2,1,0:T(8,128)}), f32[8,520,128]{2,1,0:T(8,128)S(1)}, u32[]{:S(2)}, u32[]{:S(2)}) async-start(f32[8,520,128]{2,1,0:T(8,128)} %pack.1), calls=%async_computation | async-start | bytes 4259840 | tf_op jit(solution)/shard_map/all_to_all | solution.py:172
  20.9 0.0 all-gather.3.cloned.1.call-start
  21.0 0.7 all-gather.3.cloned.1.call-update
  21.7 27.3 %all-to-all-done.tiles_ref = f32[8,520,128]{2,1,0:T(8,128)S(1)} async-done(((f32[8,520,128]{2,1,0:T(8,128)}), f32[8,520,128]{2,1,0:T(8,128)S(1)}, u32[]{:S(2)}, u32[]{:S(2)}) %all-to-all-start) | async-done | bytes 2129952 | tf_op jit(solution)/shard_map/all_to_all | solution.py:172
  49.0 0.6 slice_convert_fusion
  49.6 0.7 copy-done
  50.3 3.4 %mirror.1 = f32[16,32,512]{2,1,0:T(8,128)} custom-call(s32[8,8]{1,0:T(8,128)} %bitcast.10, f32[8,520,128]{2,1,0:T(8,128)} %copy-done, f32[32,512]{1,0:T(8,128)} %bitcast.9), custom_call_target="tpu_custom_call" | custom-call | tf_op jit(solution)/shard_map/mirror/pallas_call | solution.py:176
  53.7 6.7 %all-to-all-start.1 = ((f32[16,32,512]{2,1,0:T(8,128)}), f32[16,32,512]{2,1,0:T(8,128)S(1)}, u32[]{:S(2)}, u32[]{:S(2)}) async-start(f32[16,32,512]{2,1,0:T(8,128)} %mirror.1), calls=%async_computation.1 | async-start | bytes 2097152 | tf_op jit(solution)/shard_map/all_to_all | solution.py:183
  60.4 12.1 %all-gather.3.cloned.1.call-done = f32[512,512]{1,0:T(8,128)} async-done(((f32[32,512]{1,0:T(8,128)}), f32[512,512]{1,0:T(8,128)}) %all-gather.3.cloned.1.call-update) | async-done | bytes 1048592 | tf_op jit(solution)/shard_map/all_gather | solution.py:153
  72.5 5.9 %all-to-all-done.1.part_ref = f32[16,32,512]{2,1,0:T(8,128)S(1)} async-done(((f32[16,32,512]{2,1,0:T(8,128)}), f32[16,32,512]{2,1,0:T(8,128)S(1)}, u32[]{:S(2)}, u32[]{:S(2)}) %all-to-all-start.1) | async-done | bytes 1048608 | tf_op jit(solution)/shard_map/all_to_all | solution.py:183
  78.4 1.0 copy-done.1
  79.5 4.4 %direct.1 = f32[8,32,512]{2,1,0:T(8,128)} custom-call(s32[8,8]{1,0:T(8,128)} %bitcast.11, f32[8,520,128]{2,1,0:T(8,128)} %copy-done, f32[16,32,512]{2,1,0:T(8,128)} %bitcast.7, f32[16,32,512]{2,1,0:T(8,128)} %copy-done.1), custom_call_target="tpu_custom_call" | custom-call | tf_op jit(solution)/shard_map/direct/pallas_call | solution.py:184
  83.9 3.5 %all-to-all-start.2 = ((f32[8,32,512]{2,1,0:T(8,128)}), f32[8,32,512]{2,1,0:T(8,128)S(1)}, u32[]{:S(2)}, u32[]{:S(2)}) async-start(f32[8,32,512]{2,1,0:T(8,128)} %direct.1), calls=%async_computation.2 | async-start | bytes 1048576 | tf_op jit(solution)/shard_map/all_to_all | solution.py:192
  87.4 1.4 %slice.50.side_ref = f32[8,8,128]{2,1,0:T(8,128)} slice(f32[8,520,128]{2,1,0:T(8,128)} %copy-done), slice={[0:8], [512:520], [0:128]} | slice | bytes 65536 | tf_op jit(solution)/shard_map/slice | solution.py:174
  88.8 8.7 %all-to-all-done.2.y_ref = f32[8,32,512]{2,1,0:T(8,128)S(1)} async-done(((f32[8,32,512]{2,1,0:T(8,128)}), f32[8,32,512]{2,1,0:T(8,128)S(1)}, u32[]{:S(2)}, u32[]{:S(2)}) %all-to-all-start.2) | async-done | bytes 524320 | tf_op jit(solution)/shard_map/all_to_all | solution.py:192
  97.4 0.8 copy-done.2
  98.2 3.1 %main.1 = (f32[32,512]{1,0:T(8,128)}, f32[2,128]{1,0:T(2,128)}, f32[16,40,256]{2,1,0:T(8,128)}) custom-call(f32[8,32,512]{2,1,0:T(8,128)} %copy-done.2, f32[256,256]{1,0:T(8,128)} %w_ref.1, f32[8,8,128]{2,1,0:T(8,128)} %slice.50.side_ref, s32[1,128]{1,0:T(1,128)} %ports_ref.1, f32[2,128]{1,0:T(2,128)} %targets_ref.1), custom_call_target="tpu_custom_call" | custom-call | tf_op jit(solution)/shard_map/main/pallas_call | solution.py:194
  101.4 18.1 %all_to_all.20.parts_ref = f32[16,40,256]{2,1,0:T(8,128)} all-to-all(f32[16,40,256]{2,1,0:T(8,128)} %get-tuple-element.37), channel_id=1, replica_groups=mesh['row'=16,'col'=8] {'row'}, dimensions={0} | all-to-all | bytes 1310720 | tf_op jit(solution)/shard_map/all_to_all | solution.py:211
  119.5 1.7 %final.1 = (f32[32,256]{1,0:T(8,128)}, f32[1,32]{1,0:T(1,128)}, f32[2,32]{1,0:T(2,128)}) custom-call(f32[16,40,256]{2,1,0:T(8,128)} %all_to_all.20.parts_ref), custom_call_target="tpu_custom_call" | custom-call | tf_op jit(solution)/shard_map/final/pallas_call | solution.py:212
  (3 shorter events, 0.0 us)
Async XLA Ops:
  9.9 0.6 copy-start.3
  14.6 34.4 %all-to-all-start = ((f32[8,520,128]{2,1,0:T(8,128)}), f32[8,520,128]{2,1,0:T(8,128)S(1)}, u32[]{:S(2)}, u32[]{:S(2)}) async-start(f32[8,520,128]{2,1,0:T(8,128)} %pack.1), calls=%async_computation | async-start | bytes 4259840 | tf_op jit(solution)/shard_map/all_to_all | solution.py:172
  20.9 51.6 %all-gather.3.cloned.1.call-start = ((), (), s32[]{:S(2)}) async-start(), calls=%async_computation.4 | async-start | bytes 1114112 | tf_op jit(solution)/shard_map/all_gather | solution.py:153
  49.0 1.3 %copy-start = (f32[8,520,128]{2,1,0:T(8,128)}, f32[8,520,128]{2,1,0:T(8,128)S(1)}, u32[]{:S(2)}) copy-start(f32[8,520,128]{2,1,0:T(8,128)S(1)} %all-to-all-done.tiles_ref) | copy-start | bytes 6389764
  53.7 24.8 %all-to-all-start.1 = ((f32[16,32,512]{2,1,0:T(8,128)}), f32[16,32,512]{2,1,0:T(8,128)S(1)}, u32[]{:S(2)}, u32[]{:S(2)}) async-start(f32[16,32,512]{2,1,0:T(8,128)} %mirror.1), calls=%async_computation.1 | async-start | bytes 2097152 | tf_op jit(solution)/shard_map/all_to_all | solution.py:183
  78.4 1.0 copy-start.1
  83.9 13.6 %all-to-all-start.2 = ((f32[8,32,512]{2,1,0:T(8,128)}), f32[8,32,512]{2,1,0:T(8,128)S(1)}, u32[]{:S(2)}, u32[]{:S(2)}) async-start(f32[8,32,512]{2,1,0:T(8,128)} %direct.1), calls=%async_computation.2 | async-start | bytes 1048576 | tf_op jit(solution)/shard_map/all_to_all | solution.py:192
  97.4 0.8 copy-start.2
Sparse Core Ops, SparseCore 0:
  24.2 48.2 all-gather.2

commit v2 on v1

v2 whole, which is shorter than its diff:
```python
import functools

import jax
import jax.numpy as jnp
from jax import lax
from jax.experimental import pallas as pl
from jax.experimental.pallas import tpu as pltpu
from jax.sharding import PartitionSpec as P

F32 = jnp.float32
BF16 = jnp.bfloat16
VMEM = pl.BlockSpec(memory_space=pltpu.VMEM)
SMEM = pl.BlockSpec(memory_space=pltpu.SMEM)
NN = (((1,), (0,)), ((), ()))
NT = (((1,), (1,)), ((), ()))


def split(x):
    high = x.astype(BF16)
    low = (x - high.astype(F32)).astype(BF16)
    return high, low


def dot(a, b, dims):
    return lax.dot_general(a, b, dims, preferred_element_type=F32)


def dot3(a, b, dims):
    return dot(a[0], b[0], dims) + (dot(a[1], b[0], dims) + dot(a[0], b[1], dims))


def tile_dot(x, u, dims):
    rows = x[0].shape[0]
    wide = 1 if dims == NN else 0
    edge = u[0].shape[wide]
    every = dot(jnp.concatenate(x, axis=0), jnp.concatenate(u, axis=wide), dims)
    return every[:rows, :edge] + (every[rows:, :edge] + every[:rows, edge:] + every[rows:, edge:])


def pack_kernel(slots, rows_ref, cols_ref, count_ref, tiles_ref, bias_ref, readout_ref, out_ref, buf, sems):
    edge = tiles_ref.shape[2]
    block = bias_ref.shape[1]
    outs = readout_ref.shape[0]
    base = slots * edge
    copies = []
    for c in range(out_ref.shape[0]):
        here = out_ref.at[c, pl.ds(0, base), :]
        copies.append(pltpu.make_async_copy(tiles_ref.at[0], here, sems.at[0, c]))
        copies[-1].start()
    lane = lax.broadcasted_iota(jnp.int32, (1, edge), 1)
    meta = jnp.where(lane == 2 * slots, count_ref[0, 0], 0)
    for k in range(slots):
        meta = jnp.where(lane == k, rows_ref[0, 0, k], meta)
        meta = jnp.where(lane == slots + k, cols_ref[0, 0, k], meta)
    buf[...] = jnp.zeros(buf.shape, F32)
    buf[0:1, :] = meta.astype(F32)
    buf[1:2, :block] = bias_ref[...]
    buf[2 : 2 + outs, :block] = readout_ref[...]
    for c in range(out_ref.shape[0]):
        copies.append(pltpu.make_async_copy(buf, out_ref.at[c, pl.ds(base, 8), :], sems.at[1, c]))
        copies[-1].start()
    for copy in copies:
        copy.wait()


def read_meta(slots, tiles_ref, meta, sem):
    edge = tiles_ref.shape[2]
    copy = pltpu.make_async_copy(tiles_ref.at[:, pl.ds(slots * edge, 8), :], meta, sem)
    copy.start()
    return copy


def slot_of(slots, meta, d, k):
    row, col, count = [meta[d, 0, at].astype(jnp.int32) for at in (k, slots + k, 2 * slots)]
    return row, col, k < count


def mirror_kernel(slots, tiles_ref, x_ref, keep_ref, send_ref, side_ref, copy_ref, total, meta, sem, copy_sem):
    edge = tiles_ref.shape[2]
    row_tiles = x_ref.shape[1] // edge
    core = lax.axis_index("row") % 2
    copy = read_meta(slots, tiles_ref, meta, sem)
    spare = pltpu.make_async_copy(tiles_ref, copy_ref, copy_sem)
    spare.start()
    total[...] = jnp.zeros_like(total)
    side_ref[...] = tiles_ref[:, slots * edge :, :]
    copy.wait()
    for d in range(tiles_ref.shape[0]):
        for k in range(slots):
            row, col, live = slot_of(slots, meta, d, k)
            x = x_ref[:, pl.ds(pl.multiple_of(row * edge, edge), edge)]
            x = split(jnp.where(live, x, 0.0))
            u = split(tiles_ref[d, k * edge : (k + 1) * edge, :])
            lanes = pl.ds(pl.multiple_of((col % row_tiles) * edge, edge), edge)
            piece = col // row_tiles
            total[(piece % 2) ^ core, piece // 2, :, lanes] += tile_dot(x, u, NN)
    keep_ref[...] = total[0]
    send_ref[...] = total[1]
    spare.wait()


def add_kernel(a_ref, b_ref, out_ref):
    total = a_ref[...] + b_ref[...]
    if out_ref.shape == a_ref.shape:
        out_ref[...] = total
    else:
        for p in range(out_ref.shape[0]):
            out_ref[p] = total


def xor_steps(rows):
    return [2, 4, 8, 1] if rows == 16 else [1 << i for i in range(rows.bit_length() - 2, -1, -1)]


def xor_slots(rows):
    pieces = [[0]]
    for bit in xor_steps(rows):
        pieces.append([mask ^ bit for piece in pieces for mask in piece])
    return pieces


def xor_exchange(x, bit, rows):
    return lax.ppermute(x, "row", [(i, i ^ bit) for i in range(rows)])


def direct_kernel(slots, *refs):
    tiles_ref, pieces, out_ref, x_all, meta, sem = refs[0], refs[1:-4], refs[-4], refs[-3], refs[-2], refs[-1]
    me = lax.axis_index("row")
    edge = tiles_ref.shape[2]
    row_tiles = out_ref.shape[1] // edge
    copy = read_meta(slots, tiles_ref, meta, sem)
    out_ref[...] = jnp.zeros_like(out_ref)
    for piece, slots_of in zip(pieces, xor_slots(x_all.shape[0])):
        for at, slot in enumerate(slots_of):
            x_all[slot] = piece[at]
    copy.wait()
    for d in range(tiles_ref.shape[0]):
        for k in range(slots):
            row, col, live = slot_of(slots, meta, d, k)
            lanes = pl.ds(pl.multiple_of((col % row_tiles) * edge, edge), edge)
            x = split(jnp.where(live, x_all[(col // row_tiles) ^ me, :, lanes], 0.0))
            u = split(tiles_ref[d, k * edge : (k + 1) * edge, :])
            here = pl.ds(pl.multiple_of(row * edge, edge), edge)
            out_ref[:, here] += tile_dot(x, u, NT)


def gather_sum_kernel(part_ref, direct_ref, out_ref):
    total = direct_ref[...]
    for r in range(part_ref.shape[0]):
        total = total + part_ref[r]
    for c in range(out_ref.shape[0]):
        out_ref[c] = total


def prep_kernel(w_ref, side_ref, wt_ref, side_t_ref, readout_ref):
    wt = split(w_ref[...].T)
    wt_ref[0] = wt[0]
    wt_ref[1] = wt[1]
    cols = side_ref.shape[0]
    block = w_ref.shape[0] // cols
    for c in range(cols):
        side = side_ref[c]
        side_t_ref[c * block : (c + 1) * block, :] = side.T[:block, :]
        readout_ref[:, c * block : (c + 1) * block] = side[:, :block]


def ports_kernel(
    y_ref, wt_ref, side_t_ref, readout_ref, ports_ref, targets_ref, pred_ref, grad_ref, pre_p, hid_p
):
    me = lax.axis_index("col")
    cols, block, nodes = y_ref.shape
    feats = cols * block
    mine = pl.ds(pl.multiple_of(me * block, block), block)
    y = split(y_ref[...].reshape(feats, nodes))
    node = lax.broadcasted_iota(jnp.int32, (nodes, ports_ref.shape[1]), 0)
    pick = (node == ports_ref[...]).astype(BF16)
    yp = split(dot(y[0], pick, NN) + dot(y[1], pick, NN))
    pre_all = dot3((wt_ref[0], wt_ref[1]), yp, NN) + side_t_ref[:, 1:2]
    pre_p[...] = pre_all
    hid_all = pre_all * jax.nn.sigmoid(pre_all)
    hid_p[...] = hid_all
    outs = targets_ref.shape[0]
    pred = dot3(split(readout_ref[...]), split(hid_all), NN)[2 : 2 + outs]
    pred_ref[...] = pred
    err = pred - targets_ref[...]
    gow = dot3(split(err), split(hid_p[mine, :]), NT)
    pre_c = pre_p[mine, :]
    s = jax.nn.sigmoid(pre_c)
    port_grad = side_t_ref[mine, 2:3] * err[0:1, :] + side_t_ref[mine, 3:4] * err[1:2, :]
    grad_pre = port_grad * (s * (1.0 + pre_c * (1.0 - s)))
    gp = split(grad_pre)
    ones = jnp.ones((1, grad_pre.shape[1]), BF16)
    gb = dot(ones, gp[0], NT) + dot(ones, gp[1], NT)
    gw = dot3(gp, yp, NT)
    grad_ref[:block, :] = gw
    grad_ref[block:, :] = jnp.zeros((grad_ref.shape[0] - block, feats), F32)
    grad_ref[block : block + outs, :block] = gow
    grad_ref[block + outs : block + outs + 1, :block] = gb


def hidden_kernel(y_ref, wt_ref, side_t_ref, hidden_ref):
    me = lax.axis_index("col")
    cols, block, nodes = y_ref.shape
    mine = pl.ds(pl.multiple_of(me * block, block), block)
    y = split(y_ref[...].reshape(cols * block, nodes))
    pre = dot3((wt_ref[0, mine, :], wt_ref[1, mine, :]), y, NN) + side_t_ref[mine, 1:2]
    hidden_ref[...] = pre * jax.nn.sigmoid(pre)


def final_kernel(parts_ref, gw_ref, gb_ref, gow_ref):
    block = gw_ref.shape[0]
    outs = gow_ref.shape[0]
    total = parts_ref[0]
    for r in range(1, parts_ref.shape[0]):
        total = total + parts_ref[r]
    gw_ref[...] = total[:block, :]
    gow_ref[...] = total[block : block + outs, :block]
    gb_ref[...] = total[block + outs : block + outs + 1, :block]


def on_chip(x):
    return pltpu.with_memory_space_constraint(x, pltpu.VMEM)


def per_device(
    features,
    weight,
    layer_bias,
    out_weight,
    adj_tiles,
    tile_rows,
    tile_cols,
    tile_count,
    port_rows,
    targets,
):
    rows = lax.axis_size("row")
    cols = lax.axis_size("col")
    nodes, block = features.shape
    feats = weight.shape[0]
    slots, edge = adj_tiles.shape[2:4]
    outs = out_weight.shape[0]
    x_own = features.T
    base = slots * edge
    length = base + 8

    anywhere = pl.BlockSpec(memory_space=pl.ANY)
    packed = pl.pallas_call(
        functools.partial(pack_kernel, slots),
        in_specs=[SMEM, SMEM, SMEM, VMEM, VMEM, VMEM],
        out_specs=anywhere,
        out_shape=jax.ShapeDtypeStruct((cols, length, edge), F32),
        scratch_shapes=[pltpu.VMEM((8, edge), F32), pltpu.SemaphoreType.DMA((2, cols))],
        name="pack",
    )(tile_rows, tile_cols, tile_count, adj_tiles.reshape(1, base, edge), layer_bias[None, :], out_weight)
    steps = xor_steps(rows)
    first = xor_exchange(x_own[None], steps[0], rows)
    packed, first = lax.optimization_barrier((packed, first))
    tiles = on_chip(lax.all_to_all(packed, "col", 0, 0))
    pieces = [x_own[None], first]
    for bit in steps[1:]:
        pieces.append(xor_exchange(jnp.concatenate(pieces, axis=0), bit, rows))
    x_first, pieces[-1] = lax.optimization_barrier((x_own, pieces[-1]))

    meta = [pltpu.SMEM((cols, 8, edge), F32), pltpu.SemaphoreType.DMA]
    half = (rows // 2, block, nodes)
    keep, send, sides, spare_tiles = pl.pallas_call(
        functools.partial(mirror_kernel, slots),
        in_specs=[VMEM, VMEM],
        out_specs=[VMEM] * 3 + [anywhere],
        out_shape=[
            pltpu.VMEM(half, F32),
            pltpu.VMEM(half, F32),
            pltpu.VMEM((cols, 8, edge), F32),
            jax.ShapeDtypeStruct((cols, length, edge), F32),
        ],
        scratch_shapes=[pltpu.VMEM((2,) + half, F32)] + meta + [pltpu.SemaphoreType.DMA],
        name="mirror",
    )(tiles, x_first)
    other_core = [(r, r ^ 1) for r in range(rows)]
    chips = [list(range(core, rows, 2)) for core in range(2)]
    paired = pl.pallas_call(
        add_kernel,
        in_specs=[VMEM, VMEM],
        out_specs=VMEM,
        out_shape=pltpu.VMEM(half, F32),
        name="pair_sum",
    )(on_chip(keep), on_chip(lax.ppermute(send, "row", other_core)))
    parts = on_chip(lax.all_to_all(paired, "row", 0, 0, axis_index_groups=chips))
    direct = pl.pallas_call(
        functools.partial(direct_kernel, slots),
        in_specs=[VMEM] * (1 + len(pieces)),
        out_specs=VMEM,
        out_shape=pltpu.VMEM((block, nodes), F32),
        scratch_shapes=[pltpu.VMEM((rows, block, nodes), F32)] + meta,
        name="direct",
    )(spare_tiles, *pieces)
    wt, side_t, readout = pl.pallas_call(
        prep_kernel,
        in_specs=[VMEM] * 2,
        out_specs=[VMEM] * 3,
        out_shape=[
            pltpu.VMEM((2, feats, feats), BF16),
            pltpu.VMEM((feats, 8), F32),
            pltpu.VMEM((8, feats), F32),
        ],
        name="prep",
    )(weight, on_chip(sides))
    wt, side_t, readout = on_chip(wt), on_chip(side_t), on_chip(readout)
    y_own = pl.pallas_call(
        gather_sum_kernel,
        in_specs=[VMEM, VMEM],
        out_specs=VMEM,
        out_shape=pltpu.VMEM((cols, block, nodes), F32),
        name="gather_sum",
    )(parts, on_chip(direct))
    y = on_chip(lax.all_to_all(y_own, "col", 0, 0))
    ports = port_rows.shape[1]
    predictions, grads = pl.pallas_call(
        ports_kernel,
        in_specs=[VMEM] * 6,
        out_specs=[VMEM, VMEM],
        out_shape=[
            jax.ShapeDtypeStruct((outs, ports), F32),
            pltpu.VMEM((block + 8, feats), F32),
        ],
        scratch_shapes=[pltpu.VMEM((feats, ports), F32)] * 2,
        name="ports",
    )(y, wt, side_t, readout, port_rows, targets)
    pair_grads = pl.pallas_call(
        add_kernel,
        in_specs=[VMEM, VMEM],
        out_specs=VMEM,
        out_shape=pltpu.VMEM((rows // 2, block + 8, feats), F32),
        name="pair_grads",
    )(on_chip(grads), on_chip(lax.ppermute(grads, "row", other_core)))
    all_grads = on_chip(lax.all_to_all(pair_grads, "row", 0, 0, axis_index_groups=chips))
    hidden_t = pl.pallas_call(
        hidden_kernel,
        in_specs=[VMEM] * 3,
        out_specs=VMEM,
        out_shape=jax.ShapeDtypeStruct((block, nodes), F32),
        name="hidden",
    )(y, wt, side_t)
    gw, gb, gow = pl.pallas_call(
        final_kernel,
        in_specs=[VMEM],
        out_specs=[VMEM] * 3,
        out_shape=[
            jax.ShapeDtypeStruct((block, feats), F32),
            jax.ShapeDtypeStruct((1, block), F32),
            jax.ShapeDtypeStruct((outs, block), F32),
        ],
        name="final",
    )(all_grads)
    return (hidden_t.T, predictions, gw.T, gb[0], gow)


def solution(mesh):
    placed = (
        P("row", "col"),
        P(),
        P("col"),
        P(None, "col"),
        P("row", "col", None, None, None),
        P("row", "col", None),
        P("row", "col", None),
        P("row", "col"),
        P("row", None),
        P(None, "row"),
    )
    return jax.shard_map(
        per_device,
        mesh=mesh,
        in_specs=placed,
        out_specs=(P("row", "col"), P(None, "row"), P(None, "col"), P("col"), P(None, "col")),
        check_vma=False,
    )
```

time: 129 us -> 95.7 us (0.74)
  blocking collectives: 18.1 us -> 0 us
  between operations: 14.7 us -> 1.39 us
  starting transfers between devices: 16.6 us -> 27.9 us
  waiting for transfers between devices: 54.7 us -> 48.6 us
  local copies, waits for them, and re-layouts: 6.61 us -> 0.82 us
    all_to_all x1 -> x0, blocking collectives: 18.1 us -> none  [per_device(): all_grads = lax.all_to_all(grads, 'row', 0, 0)]
    ppermute x0 -> x6, waiting for transfers between devices: none -> 13.2 us  [the longest x4 10.1 us: xor_exchange(): return lax.ppermute(x, 'row', [(i, i ^ bit) for i in range(rows)])]
    all_gather x1 -> x0, waiting for transfers between devices: 12.1 us -> none  [per_device(): x_all = lax.all_gather(x_own, 'row', axis=0)]
    ppermute x0 -> x6, starting transfers between devices: none -> 8.29 us  [the longest x4 8.2 us: xor_exchange(): return lax.ppermute(x, 'row', [(i, i ^ bit) for i in range(rows)])]
    all_to_all x3 -> x4, waiting for transfers between devices: 41.9 us -> 35.4 us  [the longest x1 10.4 us: per_device(): tiles = on_chip(lax.all_to_all(packed, 'col', 0, 0))]
    all_to_all x3 -> x4, starting transfers between devices: 16.6 us -> 19.6 us  [the longest x1 6.43 us: per_device(): lax.all_to_all(paired, 'row', 0, 0, axis_index_groups=chips)]
    unnamed x8 -> x10, local copies, waits for them, and re-layouts: 3.11 us -> 0.82 us
    scatter x2 -> x0, local copies, waits for them, and re-layouts: 2.13 us -> none  [per_device(): side.at[1, :block].set(layer_bias).at[2:2 + outs, :block].set(out_weight)]
  transfers between devices with their start and end apart: 4 -> 10, of which waited for: 4 -> 9; matrix products, arithmetic and copies ran while one was open for 2% -> 0% of each run, Pallas kernels for 3% -> 9%
where the time goes in v2:
time: 95.7 us; the launch traced here: 95 us
  waiting for transfers between devices  48.6 us (51%)
  starting transfers between devices  27.9 us (29%)
  Pallas kernels  16.3 us (17%)
  between operations  1.39 us (1%)
    all_to_all x1, waiting for transfers between devices, per_device(): tiles = on_chip(lax.all_to_all(packed, 'col', 0, 0))  10.4 us
    ppermute x4, waiting for transfers between devices, xor_exchange(): return lax.ppermute(x, 'row', [(i, i ^ bit) for i in range(rows)])  10.1 us
    all_to_all x1, waiting for transfers between devices, per_device(): lax.all_to_all(pair_grads, 'row', 0, 0, axis_index_groups=chips)  8.9 us
    ppermute x4, starting transfers between devices, xor_exchange(): return lax.ppermute(x, 'row', [(i, i ^ bit) for i in range(rows)])  8.2 us
    all_to_all x1, waiting for transfers between devices, per_device(): lax.all_to_all(paired, 'row', 0, 0, axis_index_groups=chips)  8.06 us
    all_to_all x1, waiting for transfers between devices, per_device(): y = on_chip(lax.all_to_all(y_own, 'col', 0, 0))  8.04 us
    all_to_all x1, starting transfers between devices, per_device(): lax.all_to_all(paired, 'row', 0, 0, axis_index_groups=chips)  6.43 us
    all_to_all x1, starting transfers between devices, per_device(): tiles = on_chip(lax.all_to_all(packed, 'col', 0, 0))  6.02 us
  transfers between devices with their start and end apart: 10, of which 9 were waited for; matrix products, arithmetic and copies ran while one was open for 0% of the time, Pallas kernels for 9%

profile of v2, /device:TPU:0, one launch (start us, length us, event | category | flops | bytes accessed | tf_op | source)
XLA Modules:
  0.0 95.0 jit_solution(7581200331475631164)
XLA Ops:
  0.6 3.2 %collective-permute-start = (f32[1,32,512]{2,1,0:T(8,128)}, f32[1,32,512]{2,1,0:T(8,128)S(1)}, u32[]{:S(2)}, u32[]{:S(2)}) collective-permute-start(f32[1,32,512]{2,1,0:T(8,128)} %bitcast.8), channel_id=1, source_target_pairs={{0,16},{8,24},{16,0},{24,8},{32,48},{40,56},{48,32},{56,40},{64,80... | collective-permute-start | bytes 196616 | tf_op jit(solution)/shard_map/ppermute | solution.py:123
  4.5 2.5 %pack.1 = f32[8,520,128]{2,1,0:T(8,128)} custom-call(s32[1,1,4]{2,1,0:T(1,128)} %rows_ref.1, s32[1,1,4]{2,1,0:T(1,128)} %cols_ref.1, s32[1,1]{1,0:T(1,128)S(6)} %copy.15.count_ref, f32[1,512,128]{2,1,0:T(8,128)} %bitcast.14, f32[1,32]{1,0:T(1,128)} %bitcast.16, f32[2,32]{1,0:T(2,128)} %readout_ref.1), custom_call_target="tpu_custom_call" | custom-call | tf_op jit(solution)/shard_map/pack/pallas_call | solution.py:248
  7.0 6.0 %all-to-all-start = ((f32[8,520,128]{2,1,0:T(8,128)}), f32[8,520,128]{2,1,0:T(8,128)S(1)}, u32[]{:S(2)}, u32[]{:S(2)}) async-start(f32[8,520,128]{2,1,0:T(8,128)} %pack.1), calls=%async_computation | async-start | bytes 4259840 | tf_op jit(solution)/shard_map/all_to_all | solution.py:259
  13.0 1.7 %collective-permute-start.1 = (f32[2,32,512]{2,1,0:T(8,128)S(1)}, f32[2,32,512]{2,1,0:T(8,128)S(1)}, u32[]{:S(2)}, u32[]{:S(2)}) collective-permute-start(f32[2,32,512]{2,1,0:T(8,128)S(1)} %pad_maximum_fusion.2), channel_id=1, source_target_pairs={{0,32},{8,40},{16,48},{24,56},{32,0},{40,8},{48,16},{56,24},{64,96... | collective-permute-start | bytes 393224 | tf_op jit(solution)/shard_map/ppermute | solution.py:123
  14.7 3.4 %collective-permute-done.1.refs_3_ = f32[2,32,512]{2,1,0:T(8,128)S(1)} collective-permute-done((f32[2,32,512]{2,1,0:T(8,128)S(1)}, f32[2,32,512]{2,1,0:T(8,128)S(1)}, u32[]{:S(2)}, u32[]{:S(2)}) %collective-permute-start.1) | collective-permute-done | bytes 131104 | tf_op jit(solution)/shard_map/ppermute | solution.py:123
  18.1 3.3 %collective-permute-start.2 = (f32[4,32,512]{2,1,0:T(8,128)S(1)}, f32[4,32,512]{2,1,0:T(8,128)S(1)}, u32[]{:S(2)}, u32[]{:S(2)}) collective-permute-start(f32[4,32,512]{2,1,0:T(8,128)S(1)} %pad_maximum_fusion.1), channel_id=1, source_target_pairs={{0,64},{8,72},{16,80},{24,88},{32,96},{40,104},{48,112},{56,120},{... | collective-permute-start | bytes 786440 | tf_op jit(solution)/shard_map/ppermute | solution.py:123
  21.4 4.8 %collective-permute-done.2.refs_4_ = f32[4,32,512]{2,1,0:T(8,128)S(1)} collective-permute-done((f32[4,32,512]{2,1,0:T(8,128)S(1)}, f32[4,32,512]{2,1,0:T(8,128)S(1)}, u32[]{:S(2)}, u32[]{:S(2)}) %collective-permute-start.2) | collective-permute-done | bytes 262176 | tf_op jit(solution)/shard_map/ppermute | solution.py:123
  26.3 1.9 %collective-permute-done.3.refs_5_ = f32[8,32,512]{2,1,0:T(8,128)S(1)} collective-permute-done((f32[8,32,512]{2,1,0:T(8,128)S(1)}, f32[8,32,512]{2,1,0:T(8,128)S(1)}, u32[]{:S(2)}, u32[]{:S(2)}) %collective-permute-start.3) | collective-permute-done | bytes 524320 | tf_op jit(solution)/shard_map/ppermute | solution.py:123
  29.0 10.4 %all-to-all-done.tiles_ref = f32[8,520,128]{2,1,0:T(8,128)S(1)} async-done(((f32[8,520,128]{2,1,0:T(8,128)}), f32[8,520,128]{2,1,0:T(8,128)S(1)}, u32[]{:S(2)}, u32[]{:S(2)}) %all-to-all-start) | async-done | bytes 2129952 | tf_op jit(solution)/shard_map/all_to_all | solution.py:259
  39.4 2.8 %mirror.1 = (f32[8,32,512]{2,1,0:T(8,128)S(1)}, f32[8,32,512]{2,1,0:T(8,128)S(1)}, f32[8,8,128]{2,1,0:T(8,128)S(1)}, f32[8,520,128]{2,1,0:T(8,128)}) custom-call(f32[8,520,128]{2,1,0:T(8,128)S(1)} %all-to-all-done.tiles_ref, f32[32,512]{1,0:T(8,128)} %bitcast.9), custom_call_target="tpu_custom_call" | custom-call | tf_op jit(solution)/shard_map/mirror/pallas_call | solution.py:267
  42.3 1.9 %collective-permute-done.4.b_ref = f32[8,32,512]{2,1,0:T(8,128)S(1)} collective-permute-done((f32[8,32,512]{2,1,0:T(8,128)S(1)}, f32[8,32,512]{2,1,0:T(8,128)S(1)}, u32[]{:S(2)}, u32[]{:S(2)}) %collective-permute-start.4) | collective-permute-done | bytes 524320 | tf_op jit(solution)/shard_map/ppermute | solution.py:288
  44.2 0.9 pair_sum.1
  45.1 6.4 %all-to-all-start.1 = ((f32[8,32,512]{2,1,0:T(8,128)}), f32[8,32,512]{2,1,0:T(8,128)S(1)}, u32[]{:S(2)}, u32[]{:S(2)}) async-start(f32[8,32,512]{2,1,0:T(8,128)} %pair_sum.1), calls=%async_computation.1 | async-start | bytes 1048576 | tf_op jit(solution)/shard_map/all_to_all | solution.py:289
  51.5 3.8 %direct.1.direct_ref = f32[32,512]{1,0:T(8,128)S(1)} custom-call(f32[8,520,128]{2,1,0:T(8,128)} %get-tuple-element.26.refs_0_, f32[1,32,512]{2,1,0:T(8,128)} %bitcast.10, f32[1,32,512]{2,1,0:T(8,128)} %copy-done.3, f32[2,32,512]{2,1,0:T(8,128)} %copy-done.1, f32[4,32,512]{2,1,0:T(8,128)} %copy-done.2, f32[8,32,512]{2,1,0:T(8,128)} %copy-done.4), custom_call_target="tpu_custom_call" | custom-call | tf_op jit(solution)/shard_map/direct/pallas_call | solution.py:290
  55.3 8.1 %all-to-all-done.1.part_ref = f32[8,32,512]{2,1,0:T(8,128)S(1)} async-done(((f32[8,32,512]{2,1,0:T(8,128)}), f32[8,32,512]{2,1,0:T(8,128)S(1)}, u32[]{:S(2)}, u32[]{:S(2)}) %all-to-all-start.1) | async-done | bytes 524320 | tf_op jit(solution)/shard_map/all_to_all | solution.py:289
  63.4 0.9 gather_sum.1
  64.2 3.5 %all-to-all-start.2 = ((f32[8,32,512]{2,1,0:T(8,128)}), f32[8,32,512]{2,1,0:T(8,128)S(1)}, u32[]{:S(2)}, u32[]{:S(2)}) async-start(f32[8,32,512]{2,1,0:T(8,128)} %gather_sum.1), calls=%async_computation.2 | async-start | bytes 1048576 | tf_op jit(solution)/shard_map/all_to_all | solution.py:317
  67.7 1.1 %prep.1 = (bf16[2,256,256]{2,1,0:T(8,128)(2,1)S(1)}, f32[256,8]{1,0:T(8,128)S(1)}, f32[8,256]{1,0:T(8,128)S(1)}) custom-call(f32[256,256]{1,0:T(8,128)} %w_ref.1, f32[8,8,128]{2,1,0:T(8,128)S(1)} %get-tuple-element.28.side_ref), custom_call_target="tpu_custom_call" | custom-call | tf_op jit(solution)/shard_map/prep/pallas_call | solution.py:298
  68.9 8.0 %all-to-all-done.2.y_ref = f32[8,32,512]{2,1,0:T(8,128)S(1)} async-done(((f32[8,32,512]{2,1,0:T(8,128)}), f32[8,32,512]{2,1,0:T(8,128)S(1)}, u32[]{:S(2)}, u32[]{:S(2)}) %all-to-all-start.2) | async-done | bytes 524320 | tf_op jit(solution)/shard_map/all_to_all | solution.py:317
  76.9 2.0 %ports.1 = (f32[2,128]{1,0:T(2,128)}, f32[40,256]{1,0:T(8,128)S(1)}) custom-call(f32[8,32,512]{2,1,0:T(8,128)S(1)} %all-to-all-done.2.y_ref, bf16[2,256,256]{2,1,0:T(8,128)(2,1)S(1)} %get-tuple-element.29.wt_ref, f32[256,8]{1,0:T(8,128)S(1)} %get-tuple-element.30.side_t_ref, f32[8,256]{1,0:T(8,128)S(1)} %get-tuple-element.31.readout_ref, ...), custom_call_target="tpu_custom_call" | custom-call | tf_op jit(solution)/shard_map/ports/pallas_call | solution.py:319
  78.9 1.2 %collective-permute-done.5.b_ref = f32[40,256]{1,0:T(8,128)S(1)} collective-permute-done((f32[40,256]{1,0:T(8,128)S(1)}, f32[40,256]{1,0:T(8,128)S(1)}, u32[]{:S(2)}, u32[]{:S(2)}) %collective-permute-start.5) | collective-permute-done | bytes 40992 | tf_op jit(solution)/shard_map/ppermute | solution.py:336
  80.9 3.7 %all-to-all-start.3 = ((f32[8,40,256]{2,1,0:T(8,128)}), f32[8,40,256]{2,1,0:T(8,128)S(1)}, u32[]{:S(2)}, u32[]{:S(2)}) async-start(f32[8,40,256]{2,1,0:T(8,128)} %pair_grads.1), calls=%async_computation.3 | async-start | bytes 655360 | tf_op jit(solution)/shard_map/all_to_all | solution.py:337
  84.6 0.9 hidden.1
  85.5 8.9 %all-to-all-done.3.parts_ref = f32[8,40,256]{2,1,0:T(8,128)S(1)} async-done(((f32[8,40,256]{2,1,0:T(8,128)}), f32[8,40,256]{2,1,0:T(8,128)S(1)}, u32[]{:S(2)}, u32[]{:S(2)}) %all-to-all-start.3) | async-done | bytes 327712 | tf_op jit(solution)/shard_map/all_to_all | solution.py:337
  (19 shorter events, 2.4 us)
Async XLA Ops:
  0.6 6.3 %collective-permute-start = (f32[1,32,512]{2,1,0:T(8,128)}, f32[1,32,512]{2,1,0:T(8,128)S(1)}, u32[]{:S(2)}, u32[]{:S(2)}) collective-permute-start(f32[1,32,512]{2,1,0:T(8,128)} %bitcast.8), channel_id=1, source_target_pairs={{0,16},{8,24},{16,0},{24,8},{32,48},{40,56},{48,32},{56,40},{64,80... | collective-permute-start | bytes 196616 | tf_op jit(solution)/shard_map/ppermute | solution.py:123
  7.0 6.1 %copy-start = (f32[512,32]{0,1:T(8,128)S(1)}, f32[512,32]{0,1:T(8,128)}, u32[]{:S(2)}) copy-start(f32[512,32]{0,1:T(8,128)} %param.10) | copy-start | bytes 196612
  7.0 19.2 %copy-start.3 = (f32[1,32,512]{2,1,0:T(8,128)}, f32[1,32,512]{2,1,0:T(8,128)S(1)}, u32[]{:S(2)}) copy-start(f32[1,32,512]{2,1,0:T(8,128)S(1)} %collective-permute-done.refs_2_) | copy-start | bytes 196612
  7.0 32.4 %all-to-all-start = ((f32[8,520,128]{2,1,0:T(8,128)}), f32[8,520,128]{2,1,0:T(8,128)S(1)}, u32[]{:S(2)}, u32[]{:S(2)}) async-start(f32[8,520,128]{2,1,0:T(8,128)} %pack.1), calls=%async_computation | async-start | bytes 4259840 | tf_op jit(solution)/shard_map/all_to_all | solution.py:259
  13.0 5.0 %collective-permute-start.1 = (f32[2,32,512]{2,1,0:T(8,128)S(1)}, f32[2,32,512]{2,1,0:T(8,128)S(1)}, u32[]{:S(2)}, u32[]{:S(2)}) collective-permute-start(f32[2,32,512]{2,1,0:T(8,128)S(1)} %pad_maximum_fusion.2), channel_id=1, source_target_pairs={{0,32},{8,40},{16,48},{24,56},{32,0},{40,8},{48,16},{56,24},{64,96... | collective-permute-start | bytes 393224 | tf_op jit(solution)/shard_map/ppermute | solution.py:123
  18.1 27.0 %copy-start.1 = (f32[2,32,512]{2,1,0:T(8,128)}, f32[2,32,512]{2,1,0:T(8,128)S(1)}, u32[]{:S(2)}) copy-start(f32[2,32,512]{2,1,0:T(8,128)S(1)} %collective-permute-done.1.refs_3_) | copy-start | bytes 393220
  18.1 8.0 %collective-permute-start.2 = (f32[4,32,512]{2,1,0:T(8,128)S(1)}, f32[4,32,512]{2,1,0:T(8,128)S(1)}, u32[]{:S(2)}, u32[]{:S(2)}) collective-permute-start(f32[4,32,512]{2,1,0:T(8,128)S(1)} %pad_maximum_fusion.1), channel_id=1, source_target_pairs={{0,64},{8,72},{16,80},{24,88},{32,96},{40,104},{48,112},{56,120},{... | collective-permute-start | bytes 786440 | tf_op jit(solution)/shard_map/ppermute | solution.py:123
  26.2 2.0 %copy-start.2 = (f32[4,32,512]{2,1,0:T(8,128)}, f32[4,32,512]{2,1,0:T(8,128)S(1)}, u32[]{:S(2)}) copy-start(f32[4,32,512]{2,1,0:T(8,128)S(1)} %collective-permute-done.2.refs_4_) | copy-start | bytes 786436
  26.2 2.0 %collective-permute-start.3 = (f32[8,32,512]{2,1,0:T(8,128)S(1)}, f32[8,32,512]{2,1,0:T(8,128)S(1)}, u32[]{:S(2)}, u32[]{:S(2)}) collective-permute-start(f32[8,32,512]{2,1,0:T(8,128)S(1)} %pad_maximum_fusion), channel_id=1, source_target_pairs={{0,8},{8,0},{16,24},{24,16},{32,40},{40,32},{48,56},{56,48},{64,72... | collective-permute-start | bytes 1572872 | tf_op jit(solution)/shard_map/ppermute | solution.py:123
  28.2 0.8 copy-start.4
  42.2 2.0 %collective-permute-start.4 = (f32[8,32,512]{2,1,0:T(8,128)S(1)}, f32[8,32,512]{2,1,0:T(8,128)S(1)}, u32[]{:S(2)}, u32[]{:S(2)}) collective-permute-start(f32[8,32,512]{2,1,0:T(8,128)S(1)} %get-tuple-element.25), channel_id=1, source_target_pairs={{0,8},{8,0},{16,24},{24,16},{32,40},{40,32},{48,56},{56,48},{64,72... | collective-permute-start | bytes 1572872 | tf_op jit(solution)/shard_map/ppermute | solution.py:288
  45.1 18.3 %all-to-all-start.1 = ((f32[8,32,512]{2,1,0:T(8,128)}), f32[8,32,512]{2,1,0:T(8,128)S(1)}, u32[]{:S(2)}, u32[]{:S(2)}) async-start(f32[8,32,512]{2,1,0:T(8,128)} %pair_sum.1), calls=%async_computation.1 | async-start | bytes 1048576 | tf_op jit(solution)/shard_map/all_to_all | solution.py:289
  64.2 12.7 %all-to-all-start.2 = ((f32[8,32,512]{2,1,0:T(8,128)}), f32[8,32,512]{2,1,0:T(8,128)S(1)}, u32[]{:S(2)}, u32[]{:S(2)}) async-start(f32[8,32,512]{2,1,0:T(8,128)} %gather_sum.1), calls=%async_computation.2 | async-start | bytes 1048576 | tf_op jit(solution)/shard_map/all_to_all | solution.py:317
  78.9 1.2 %collective-permute-start.5 = (f32[40,256]{1,0:T(8,128)S(1)}, f32[40,256]{1,0:T(8,128)S(1)}, u32[]{:S(2)}, u32[]{:S(2)}) collective-permute-start(f32[40,256]{1,0:T(8,128)S(1)} %get-tuple-element.33.a_ref), channel_id=1, source_target_pairs={{0,8},{8,0},{16,24},{24,16},{32,40},{40,32},{48,56},{56,48},{64,72... | collective-permute-start | bytes 122888 | tf_op jit(solution)/shard_map/ppermute | solution.py:336
  80.9 13.5 %all-to-all-start.3 = ((f32[8,40,256]{2,1,0:T(8,128)}), f32[8,40,256]{2,1,0:T(8,128)S(1)}, u32[]{:S(2)}, u32[]{:S(2)}) async-start(f32[8,40,256]{2,1,0:T(8,128)} %pair_grads.1), calls=%async_computation.3 | async-start | bytes 655360 | tf_op jit(solution)/shard_map/all_to_all | solution.py:337

commit v3 on v2

--- a/solution.py
+++ b/solution.py
@@ -13,6 +13,7 @@
 SMEM = pl.BlockSpec(memory_space=pltpu.SMEM)
 NN = (((1,), (0,)), ((), ()))
 NT = (((1,), (1,)), ((), ()))
+TILE_ORDER = [5, 1, 7, 3, 4, 2, 6]
 
 
 def split(x):
@@ -37,37 +38,29 @@
     return every[:rows, :edge] + (every[rows:, :edge] + every[:rows, edge:] + every[rows:, edge:])
 
 
-def pack_kernel(slots, rows_ref, cols_ref, count_ref, tiles_ref, bias_ref, readout_ref, out_ref, buf, sems):
+def pack_kernel(slots, rows_ref, cols_ref, count_ref, tiles_ref, bias_ref, readout_ref, out_ref, own_ref):
     edge = tiles_ref.shape[2]
     block = bias_ref.shape[1]
     outs = readout_ref.shape[0]
     base = slots * edge
-    copies = []
-    for c in range(out_ref.shape[0]):
-        here = out_ref.at[c, pl.ds(0, base), :]
-        copies.append(pltpu.make_async_copy(tiles_ref.at[0], here, sems.at[0, c]))
-        copies[-1].start()
+    out_ref[:base, :] = tiles_ref[0]
     lane = lax.broadcasted_iota(jnp.int32, (1, edge), 1)
     meta = jnp.where(lane == 2 * slots, count_ref[0, 0], 0)
     for k in range(slots):
         meta = jnp.where(lane == k, rows_ref[0, 0, k], meta)
         meta = jnp.where(lane == slots + k, cols_ref[0, 0, k], meta)
-    buf[...] = jnp.zeros(buf.shape, F32)
-    buf[0:1, :] = meta.astype(F32)
-    buf[1:2, :block] = bias_ref[...]
-    buf[2 : 2 + outs, :block] = readout_ref[...]
-    for c in range(out_ref.shape[0]):
-        copies.append(pltpu.make_async_copy(buf, out_ref.at[c, pl.ds(base, 8), :], sems.at[1, c]))
-        copies[-1].start()
+    out_ref[base : base + 8, :] = jnp.zeros((8, edge), F32)
+    out_ref[base : base + 1, :] = meta.astype(F32)
+    out_ref[base + 1 : base + 2, :block] = bias_ref[...]
+    out_ref[base + 2 : base + 2 + outs, :block] = readout_ref[...]
+    own_ref[...] = out_ref[...]
+
+
+def start_all(pairs, sems):
+    copies = [pltpu.make_async_copy(src, dst, sems.at[i]) for i, (src, dst) in enumerate(pairs)]
     for copy in copies:
-        copy.wait()
-
-
-def read_meta(slots, tiles_ref, meta, sem):
-    edge = tiles_ref.shape[2]
-    copy = pltpu.make_async_copy(tiles_ref.at[:, pl.ds(slots * edge, 8), :], meta, sem)
-    copy.start()
-    return copy
+        copy.start()
+    return copies
 
 
 def slot_of(slots, meta, d, k):
@@ -75,28 +68,32 @@
     return row, col, k < count
 
 
-def mirror_kernel(slots, tiles_ref, x_ref, keep_ref, send_ref, side_ref, copy_ref, total, meta, sem, copy_sem):
-    edge = tiles_ref.shape[2]
+def mirror_kernel(slots, order, *refs):
+    tiles_refs, refs = refs[: len(order)], refs[len(order) :]
+    x_ref, keep_ref, send_ref, side_ref, copy_ref, total, meta, meta_sems, copy_sems = refs
+    edge = tiles_refs[0].shape[1]
+    base = slots * edge
     row_tiles = x_ref.shape[1] // edge
     core = lax.axis_index("row") % 2
-    copy = read_meta(slots, tiles_ref, meta, sem)
-    spare = pltpu.make_async_copy(tiles_ref, copy_ref, copy_sem)
-    spare.start()
+    metas = start_all([(ref.at[pl.ds(base, 8), :], meta.at[d]) for d, ref in enumerate(tiles_refs)], meta_sems)
+    spares = start_all([(ref, copy_ref.at[d]) for d, ref in enumerate(tiles_refs)], copy_sems)
     total[...] = jnp.zeros_like(total)
-    side_ref[...] = tiles_ref[:, slots * edge :, :]
-    copy.wait()
-    for d in range(tiles_ref.shape[0]):
+    for d, ref in enumerate(tiles_refs):
+        side_ref[d] = ref[base:, :]
+    for d, ref in enumerate(tiles_refs):
+        metas[d].wait()
         for k in range(slots):
             row, col, live = slot_of(slots, meta, d, k)
             x = x_ref[:, pl.ds(pl.multiple_of(row * edge, edge), edge)]
             x = split(jnp.where(live, x, 0.0))
-            u = split(tiles_ref[d, k * edge : (k + 1) * edge, :])
+            u = split(ref[k * edge : (k + 1) * edge, :])
             lanes = pl.ds(pl.multiple_of((col % row_tiles) * edge, edge), edge)
             piece = col // row_tiles
             total[(piece % 2) ^ core, piece // 2, :, lanes] += tile_dot(x, u, NN)
     keep_ref[...] = total[0]
     send_ref[...] = total[1]
-    spare.wait()
+    for copy in spares:
+        copy.wait()
 
 
 def add_kernel(a_ref, b_ref, out_ref):
@@ -108,37 +105,27 @@
             out_ref[p] = total
 
 
-def xor_steps(rows):
-    return [2, 4, 8, 1] if rows == 16 else [1 << i for i in range(rows.bit_length() - 2, -1, -1)]
-
-
-def xor_slots(rows):
-    pieces = [[0]]
-    for bit in xor_steps(rows):
-        pieces.append([mask ^ bit for piece in pieces for mask in piece])
-    return pieces
-
-
-def xor_exchange(x, bit, rows):
-    return lax.ppermute(x, "row", [(i, i ^ bit) for i in range(rows)])
-
-
-def direct_kernel(slots, *refs):
-    tiles_ref, pieces, out_ref, x_all, meta, sem = refs[0], refs[1:-4], refs[-4], refs[-3], refs[-2], refs[-1]
-    me = lax.axis_index("row")
+def xor_exchange(x, bits, size, axis):
+    return lax.ppermute(x, axis, [(i, i ^ bits) for i in range(size)])
+
+
+def direct_kernel(slots, tiles_ref, own_ref, other_ref, out_ref, x_all, meta, sems):
+    core = lax.axis_index("row") % 2
     edge = tiles_ref.shape[2]
     row_tiles = out_ref.shape[1] // edge
-    copy = read_meta(slots, tiles_ref, meta, sem)
+    at_meta = pl.ds(slots * edge, 8)
+    count = tiles_ref.shape[0]
+    metas = start_all([(tiles_ref.at[d, at_meta, :], meta.at[d]) for d in range(count)], sems)
     out_ref[...] = jnp.zeros_like(out_ref)
-    for piece, slots_of in zip(pieces, xor_slots(x_all.shape[0])):
-        for at, slot in enumerate(slots_of):
-            x_all[slot] = piece[at]
-    copy.wait()
-    for d in range(tiles_ref.shape[0]):
+    x_all[0] = own_ref[...]
+    x_all[1] = other_ref[...]
+    for d in range(count):
+        metas[d].wait()
         for k in range(slots):
             row, col, live = slot_of(slots, meta, d, k)
             lanes = pl.ds(pl.multiple_of((col % row_tiles) * edge, edge), edge)
-            x = split(jnp.where(live, x_all[(col // row_tiles) ^ me, :, lanes], 0.0))
+            piece = col // row_tiles
+            x = split(jnp.where(live, x_all[(piece % 2) ^ core, piece // 2, :, lanes], 0.0))
             u = split(tiles_ref[d, k * edge : (k + 1) * edge, :])
             here = pl.ds(pl.multiple_of(row * edge, edge), edge)
             out_ref[:, here] += tile_dot(x, u, NT)
@@ -152,16 +139,18 @@
         out_ref[c] = total
 
 
-def prep_kernel(w_ref, side_ref, wt_ref, side_t_ref, readout_ref):
+def prep_kernel(order, w_ref, side_ref, wt_ref, side_t_ref, readout_ref, by_feature):
     wt = split(w_ref[...].T)
     wt_ref[0] = wt[0]
     wt_ref[1] = wt[1]
-    cols = side_ref.shape[0]
-    block = w_ref.shape[0] // cols
-    for c in range(cols):
-        side = side_ref[c]
-        side_t_ref[c * block : (c + 1) * block, :] = side.T[:block, :]
-        readout_ref[:, c * block : (c + 1) * block] = side[:, :block]
+    me = lax.axis_index("col")
+    block = w_ref.shape[0] // len(order)
+    by_feature[...] = jnp.zeros_like(by_feature)
+    for d, mask in enumerate(order):
+        here = pl.ds(pl.multiple_of((me ^ mask) * block, block), block)
+        by_feature[here, :8] = side_ref[d].T[:block, :]
+    side_t_ref[...] = by_feature[:, :8]
+    readout_ref[...] = by_feature[...].T[:8, :]
 
 
 def ports_kernel(
@@ -241,32 +230,31 @@
     slots, edge = adj_tiles.shape[2:4]
     outs = out_weight.shape[0]
     x_own = features.T
+    half = (rows // 2, block, nodes)
+    other_core = [(r, r ^ 1) for r in range(rows)]
+    chips = [list(range(core, rows, 2)) for core in range(2)]
     base = slots * edge
     length = base + 8
 
     anywhere = pl.BlockSpec(memory_space=pl.ANY)
-    packed = pl.pallas_call(
+    packed, own_tiles = pl.pallas_call(
         functools.partial(pack_kernel, slots),
         in_specs=[SMEM, SMEM, SMEM, VMEM, VMEM, VMEM],
-        out_specs=anywhere,
-        out_shape=jax.ShapeDtypeStruct((cols, length, edge), F32),
-        scratch_shapes=[pltpu.VMEM((8, edge), F32), pltpu.SemaphoreType.DMA((2, cols))],
+        out_specs=[VMEM, VMEM],
+        out_shape=[jax.ShapeDtypeStruct((length, edge), F32), pltpu.VMEM((length, edge), F32)],
         name="pack",
     )(tile_rows, tile_cols, tile_count, adj_tiles.reshape(1, base, edge), layer_bias[None, :], out_weight)
-    steps = xor_steps(rows)
-    first = xor_exchange(x_own[None], steps[0], rows)
-    packed, first = lax.optimization_barrier((packed, first))
-    tiles = on_chip(lax.all_to_all(packed, "col", 0, 0))
-    pieces = [x_own[None], first]
-    for bit in steps[1:]:
-        pieces.append(xor_exchange(jnp.concatenate(pieces, axis=0), bit, rows))
-    x_first, pieces[-1] = lax.optimization_barrier((x_own, pieces[-1]))
-
-    meta = [pltpu.SMEM((cols, 8, edge), F32), pltpu.SemaphoreType.DMA]
-    half = (rows // 2, block, nodes)
+    order = [0] + TILE_ORDER
+    tiles = [own_tiles] + [xor_exchange(packed, d, cols, "col") for d in order[1:]]
+    x_copies = jnp.broadcast_to(x_own[None], half)
+    own_rows = lax.all_to_all(x_copies, "row", 0, 0, axis_index_groups=chips)
+    other_rows = lax.ppermute(own_rows, "row", other_core)
+    tiles = [on_chip(t) for t in tiles]
+
+    meta = [pltpu.SMEM((cols, 8, edge), F32), pltpu.SemaphoreType.DMA((cols,))]
     keep, send, sides, spare_tiles = pl.pallas_call(
-        functools.partial(mirror_kernel, slots),
-        in_specs=[VMEM, VMEM],
+        functools.partial(mirror_kernel, slots, order),
+        in_specs=[VMEM] * (cols + 1),
         out_specs=[VMEM] * 3 + [anywhere],
         out_shape=[
             pltpu.VMEM(half, F32),
@@ -274,11 +262,9 @@
             pltpu.VMEM((cols, 8, edge), F32),
             jax.ShapeDtypeStruct((cols, length, edge), F32),
         ],
-        scratch_shapes=[pltpu.VMEM((2,) + half, F32)] + meta + [pltpu.SemaphoreType.DMA],
+        scratch_shapes=[pltpu.VMEM((2,) + half, F32)] + meta + [pltpu.SemaphoreType.DMA((cols,))],
         name="mirror",
-    )(tiles, x_first)
-    other_core = [(r, r ^ 1) for r in range(rows)]
-    chips = [list(range(core, rows, 2)) for core in range(2)]
+    )(*tiles, x_own)
     paired = pl.pallas_call(
         add_kernel,
         in_specs=[VMEM, VMEM],
@@ -289,14 +275,14 @@
     parts = on_chip(lax.all_to_all(paired, "row", 0, 0, axis_index_groups=chips))
     direct = pl.pallas_call(
         functools.partial(direct_kernel, slots),
-        in_specs=[VMEM] * (1 + len(pieces)),
+        in_specs=[VMEM] * 3,
         out_specs=VMEM,
         out_shape=pltpu.VMEM((block, nodes), F32),
-        scratch_shapes=[pltpu.VMEM((rows, block, nodes), F32)] + meta,
+        scratch_shapes=[pltpu.VMEM((2,) + half, F32)] + meta,
         name="direct",
-    )(spare_tiles, *pieces)
+    )(spare_tiles, on_chip(own_rows), on_chip(other_rows))
     wt, side_t, readout = pl.pallas_call(
-        prep_kernel,
+        functools.partial(prep_kernel, order),
         in_specs=[VMEM] * 2,
         out_specs=[VMEM] * 3,
         out_shape=[
@@ -304,6 +290,7 @@
             pltpu.VMEM((feats, 8), F32),
             pltpu.VMEM((8, feats), F32),
         ],
+        scratch_shapes=[pltpu.VMEM((feats, edge), F32)],
         name="prep",
     )(weight, on_chip(sides))
     wt, side_t, readout = on_chip(wt), on_chip(side_t), on_chip(readout)

time: 95.7 us -> 92.4 us (0.966)
  waiting for transfers between devices: 48.6 us -> 39.4 us
  starting transfers between devices: 27.9 us -> 32.1 us
    all_to_all x1, waiting for transfers between devices: 10.4 us -> 4.41 us  [per_device(): own_rows = lax.all_to_all(x_copies, 'row', 0, 0, axis_index_groups=chips)]
    ppermute x4 -> x8, starting transfers between devices: 8.2 us -> 13.3 us  [the longest x7 13.3 us: xor_exchange(): return lax.ppermute(x, axis, [(i, i ^ bits) for i in range(size)])]
    ppermute x1, waiting for transfers between devices: 1.9 us -> 0.01 us  [per_device(): lax.ppermute(send, 'row', other_core)]
    all_to_all x1, starting transfers between devices: 6.43 us -> 4.62 us  [per_device(): lax.all_to_all(paired, 'row', 0, 0, axis_index_groups=chips)]
    broadcast_in_dim x0 -> x1, local copies, waits for them, and re-layouts: none -> 1.7 us  [per_device(): x_copies = jnp.broadcast_to(x_own[None], half)]
    pallas_call x2, Pallas kernels: 3.94 us -> 5.2 us  [the longest x1 4.01 us: per_device(): pl.pallas_call(functools.partial(mirror_kernel, slots, order), in_specs=[...]
    ppermute x4 -> x8, waiting for transfers between devices: 10.1 us -> 9.25 us  [the longest x7 9.25 us: xor_exchange(): return lax.ppermute(x, axis, [(i, i ^ bits) for i in range(size)])]
  transfers between devices with their start and end apart: 10 -> 14, of which waited for: 9 -> 8; matrix products, arithmetic and copies ran while one was open for 0% -> 2% of each run, Pallas kernels for 9% -> 12%
where the time goes in v3:
time: 92.4 us; the launch traced here: 91.8 us
  waiting for transfers between devices  39.4 us (43%)
  starting transfers between devices  32.1 us (35%)
  Pallas kernels  17.1 us (19%)
  local copies, waits for them, and re-layouts  1.7 us (2%)
  between operations  1.34 us (1%)
    ppermute x7, starting transfers between devices, xor_exchange(): return lax.ppermute(x, axis, [(i, i ^ bits) for i in range(size)])  13.3 us
    ppermute x7, waiting for transfers between devices, xor_exchange(): return lax.ppermute(x, axis, [(i, i ^ bits) for i in range(size)])  9.25 us
    all_to_all x1, waiting for transfers between devices, per_device(): lax.all_to_all(pair_grads, 'row', 0, 0, axis_index_groups=chips)  8.9 us
    all_to_all x1, waiting for transfers between devices, per_device(): y = on_chip(lax.all_to_all(y_own, 'col', 0, 0))  8 us
    all_to_all x1, waiting for transfers between devices, per_device(): lax.all_to_all(paired, 'row', 0, 0, axis_index_groups=chips)  7.64 us
    all_to_all x1, starting transfers between devices, per_device(): own_rows = lax.all_to_all(x_copies, 'row', 0, 0, axis_index_groups=chips)  6.93 us
    all_to_all x1, starting transfers between devices, per_device(): lax.all_to_all(paired, 'row', 0, 0, axis_index_groups=chips)  4.62 us
    all_to_all x1, waiting for transfers between devices, per_device(): own_rows = lax.all_to_all(x_copies, 'row', 0, 0, axis_index_groups=chips)  4.41 us
  transfers between devices with their start and end apart: 14, of which 8 were waited for; matrix products, arithmetic and copies ran while one was open for 2% of the time, Pallas kernels for 12%

profile of v3, /device:TPU:0, one launch (start us, length us, event | category | flops | bytes accessed | tf_op | source)
XLA Modules:
  0.0 91.8 jit_solution(5999390204242499644)
XLA Ops:
  1.3 1.7 %pack.1 = (f32[520,128]{1,0:T(8,128)}, f32[520,128]{1,0:T(8,128)S(1)}) custom-call(s32[1,1,4]{2,1,0:T(1,128)} %rows_ref.1, s32[1,1,4]{2,1,0:T(1,128)} %cols_ref.1, s32[1,1]{1,0:T(1,128)S(6)} %copy.15.count_ref, f32[1,512,128]{2,1,0:T(8,128)} %bitcast.8, f32[1,32]{1,0:T(1,128)} %bitcast.10, f32[2,32]{1,0:T(2,128)} %readout_ref.1), custom_call_target="tpu_custom_call" | custom-call | tf_op jit(solution)/shard_map/pack/pallas_call | solution.py:240
  3.0 4.9 %collective-permute-start = (f32[520,128]{1,0:T(8,128)}, f32[520,128]{1,0:T(8,128)S(1)}, u32[]{:S(2)}, u32[]{:S(2)}) collective-permute-start(f32[520,128]{1,0:T(8,128)} %get-tuple-element.20), channel_id=1, source_target_pairs={{0,5},{1,4},{2,7},{3,6},{4,1},{5,0},{6,3},{7,2},{8,13},{9,12},{10,... | collective-permute-start | bytes 798728 | tf_op jit(solution)/shard_map/ppermute | solution.py:109
  8.4 1.6 %collective-permute-start.2 = (f32[520,128]{1,0:T(8,128)}, f32[520,128]{1,0:T(8,128)S(1)}, u32[]{:S(2)}, u32[]{:S(2)}) collective-permute-start(f32[520,128]{1,0:T(8,128)} %get-tuple-element.20), channel_id=1, source_target_pairs={{0,7},{1,6},{2,5},{3,4},{4,3},{5,2},{6,1},{7,0},{8,15},{9,14},{10,... | collective-permute-start | bytes 798728 | tf_op jit(solution)/shard_map/ppermute | solution.py:109
  10.4 3.6 %collective-permute-start.4 = (f32[520,128]{1,0:T(8,128)}, f32[520,128]{1,0:T(8,128)S(1)}, u32[]{:S(2)}, u32[]{:S(2)}) collective-permute-start(f32[520,128]{1,0:T(8,128)} %get-tuple-element.20), channel_id=1, source_target_pairs={{0,4},{1,5},{2,6},{3,7},{4,0},{5,1},{6,2},{7,3},{8,12},{9,13},{10,... | collective-permute-start | bytes 798728 | tf_op jit(solution)/shard_map/ppermute | solution.py:109
  14.0 1.3 %collective-permute-done.refs_1_ = f32[520,128]{1,0:T(8,128)S(1)} collective-permute-done((f32[520,128]{1,0:T(8,128)}, f32[520,128]{1,0:T(8,128)S(1)}, u32[]{:S(2)}, u32[]{:S(2)}) %collective-permute-start) | collective-permute-done | bytes 266272 | tf_op jit(solution)/shard_map/ppermute | solution.py:109
  15.3 1.6 %collective-permute-start.5 = (f32[520,128]{1,0:T(8,128)}, f32[520,128]{1,0:T(8,128)S(1)}, u32[]{:S(2)}, u32[]{:S(2)}) collective-permute-start(f32[520,128]{1,0:T(8,128)} %get-tuple-element.20), channel_id=1, source_target_pairs={{0,2},{1,3},{2,0},{3,1},{4,6},{5,7},{6,4},{7,5},{8,10},{9,11},{10,... | collective-permute-start | bytes 798728 | tf_op jit(solution)/shard_map/ppermute | solution.py:109
  16.9 4.7 %collective-permute-done.1.refs_2_ = f32[520,128]{1,0:T(8,128)S(1)} collective-permute-done((f32[520,128]{1,0:T(8,128)}, f32[520,128]{1,0:T(8,128)S(1)}, u32[]{:S(2)}, u32[]{:S(2)}) %collective-permute-start.1) | collective-permute-done | bytes 266272 | tf_op jit(solution)/shard_map/ppermute | solution.py:109
  22.3 1.7 %broadcast_in_dim.10 = f32[8,32,512]{2,1,0:T(8,128)} broadcast(f32[32,512]{1,0:T(8,128)} %bitcast.6), dimensions={1,2} | broadcast | bytes 589824 | tf_op jit(solution)/shard_map/broadcast_in_dim | solution.py:249
  24.0 6.9 %all-to-all-start.1 = ((f32[8,32,512]{2,1,0:T(8,128)}), f32[8,32,512]{2,1,0:T(8,128)}, u32[]{:S(2)}, u32[]{:S(2)}) async-start(f32[8,32,512]{2,1,0:T(8,128)} %broadcast_in_dim.10), calls=%async_computation.1 | async-start | bytes 1048576 | tf_op jit(solution)/shard_map/all_to_all | solution.py:250
  30.9 3.2 %collective-permute-done.3.refs_4_ = f32[520,128]{1,0:T(8,128)S(1)} collective-permute-done((f32[520,128]{1,0:T(8,128)}, f32[520,128]{1,0:T(8,128)S(1)}, u32[]{:S(2)}, u32[]{:S(2)}) %collective-permute-start.3) | collective-permute-done | bytes 266272 | tf_op jit(solution)/shard_map/ppermute | solution.py:109
  34.2 4.0 %mirror.1 = (f32[8,32,512]{2,1,0:T(8,128)S(1)}, f32[8,32,512]{2,1,0:T(8,128)}, f32[8,8,128]{2,1,0:T(8,128)S(1)}, f32[8,520,128]{2,1,0:T(8,128)}) custom-call(f32[520,128]{1,0:T(8,128)S(1)} %get-tuple-element.19.refs_0_, f32[520,128]{1,0:T(8,128)S(1)} %collective-permute-done.refs_1_, f32[520,128]{1,0:T(8,128)S(1)} %collective-permute-done.1.refs_2_, ...), custom_call_target="tpu_custom_call" | custom-call | tf_op jit(solution)/shard_map/mirror/pallas_call | solution.py:255
  38.3 4.4 %all-to-all-done.1.own_ref = f32[8,32,512]{2,1,0:T(8,128)} async-done(((f32[8,32,512]{2,1,0:T(8,128)}), f32[8,32,512]{2,1,0:T(8,128)}, u32[]{:S(2)}, u32[]{:S(2)}) %all-to-all-start.1) | async-done | bytes 524320 | tf_op jit(solution)/shard_map/all_to_all | solution.py:250
  42.7 0.9 pair_sum.1
  43.6 4.6 %all-to-all-start = ((f32[8,32,512]{2,1,0:T(8,128)}), f32[8,32,512]{2,1,0:T(8,128)S(1)}, u32[]{:S(2)}, u32[]{:S(2)}) async-start(f32[8,32,512]{2,1,0:T(8,128)} %pair_sum.1), calls=%async_computation | async-start | bytes 1048576 | tf_op jit(solution)/shard_map/all_to_all | solution.py:275
  48.2 4.2 %direct.1.direct_ref = f32[32,512]{1,0:T(8,128)S(1)} custom-call(f32[8,520,128]{2,1,0:T(8,128)} %get-tuple-element.23.tiles_ref, f32[8,32,512]{2,1,0:T(8,128)} %all-to-all-done.1.own_ref, f32[8,32,512]{2,1,0:T(8,128)S(1)} %collective-permute-done.8.other_ref), custom_call_target="tpu_custom_call" | custom-call | tf_op jit(solution)/shard_map/direct/pallas_call | solution.py:276
  52.4 7.6 %all-to-all-done.part_ref = f32[8,32,512]{2,1,0:T(8,128)S(1)} async-done(((f32[8,32,512]{2,1,0:T(8,128)}), f32[8,32,512]{2,1,0:T(8,128)S(1)}, u32[]{:S(2)}, u32[]{:S(2)}) %all-to-all-start) | async-done | bytes 524320 | tf_op jit(solution)/shard_map/all_to_all | solution.py:275
  60.9 3.5 %all-to-all-start.2 = ((f32[8,32,512]{2,1,0:T(8,128)}), f32[8,32,512]{2,1,0:T(8,128)S(1)}, u32[]{:S(2)}, u32[]{:S(2)}) async-start(f32[8,32,512]{2,1,0:T(8,128)} %gather_sum.1), calls=%async_computation.2 | async-start | bytes 1048576 | tf_op jit(solution)/shard_map/all_to_all | solution.py:304
  64.4 1.2 %prep.1 = (bf16[2,256,256]{2,1,0:T(8,128)(2,1)S(1)}, f32[256,8]{1,0:T(8,128)S(1)}, f32[8,256]{1,0:T(8,128)S(1)}) custom-call(f32[256,256]{1,0:T(8,128)} %w_ref.1, f32[8,8,128]{2,1,0:T(8,128)S(1)} %get-tuple-element.24.side_ref), custom_call_target="tpu_custom_call" | custom-call | tf_op jit(solution)/shard_map/prep/pallas_call | solution.py:284
  65.6 8.0 %all-to-all-done.2.y_ref = f32[8,32,512]{2,1,0:T(8,128)S(1)} async-done(((f32[8,32,512]{2,1,0:T(8,128)}), f32[8,32,512]{2,1,0:T(8,128)S(1)}, u32[]{:S(2)}, u32[]{:S(2)}) %all-to-all-start.2) | async-done | bytes 524320 | tf_op jit(solution)/shard_map/all_to_all | solution.py:304
  73.6 2.0 %ports.1 = (f32[2,128]{1,0:T(2,128)}, f32[40,256]{1,0:T(8,128)S(1)}) custom-call(f32[8,32,512]{2,1,0:T(8,128)S(1)} %all-to-all-done.2.y_ref, bf16[2,256,256]{2,1,0:T(8,128)(2,1)S(1)} %get-tuple-element.25.wt_ref, f32[256,8]{1,0:T(8,128)S(1)} %get-tuple-element.26.side_t_ref, f32[8,256]{1,0:T(8,128)S(1)} %get-tuple-element.27.readout_ref, ...), custom_call_target="tpu_custom_call" | custom-call | tf_op jit(solution)/shard_map/ports/pallas_call | solution.py:306
  75.6 1.2 %collective-permute-done.9.b_ref = f32[40,256]{1,0:T(8,128)S(1)} collective-permute-done((f32[40,256]{1,0:T(8,128)S(1)}, f32[40,256]{1,0:T(8,128)S(1)}, u32[]{:S(2)}, u32[]{:S(2)}) %collective-permute-start.9) | collective-permute-done | bytes 40992 | tf_op jit(solution)/shard_map/ppermute | solution.py:323
  77.6 3.7 %all-to-all-start.3 = ((f32[8,40,256]{2,1,0:T(8,128)}), f32[8,40,256]{2,1,0:T(8,128)S(1)}, u32[]{:S(2)}, u32[]{:S(2)}) async-start(f32[8,40,256]{2,1,0:T(8,128)} %pair_grads.1), calls=%async_computation.3 | async-start | bytes 655360 | tf_op jit(solution)/shard_map/all_to_all | solution.py:324
  81.3 0.9 hidden.1
  82.2 8.9 %all-to-all-done.3.parts_ref = f32[8,40,256]{2,1,0:T(8,128)S(1)} async-done(((f32[8,40,256]{2,1,0:T(8,128)}), f32[8,40,256]{2,1,0:T(8,128)S(1)}, u32[]{:S(2)}, u32[]{:S(2)}) %all-to-all-start.3) | async-done | bytes 327712 | tf_op jit(solution)/shard_map/all_to_all | solution.py:324
  (15 shorter events, 3.9 us)
Async XLA Ops:
  3.0 12.3 %collective-permute-start = (f32[520,128]{1,0:T(8,128)}, f32[520,128]{1,0:T(8,128)S(1)}, u32[]{:S(2)}, u32[]{:S(2)}) collective-permute-start(f32[520,128]{1,0:T(8,128)} %get-tuple-element.20), channel_id=1, source_target_pairs={{0,5},{1,4},{2,7},{3,6},{4,1},{5,0},{6,3},{7,2},{8,13},{9,12},{10,... | collective-permute-start | bytes 798728 | tf_op jit(solution)/shard_map/ppermute | solution.py:109
  7.9 13.7 %collective-permute-start.1 = (f32[520,128]{1,0:T(8,128)}, f32[520,128]{1,0:T(8,128)S(1)}, u32[]{:S(2)}, u32[]{:S(2)}) collective-permute-start(f32[520,128]{1,0:T(8,128)} %get-tuple-element.20), channel_id=1, source_target_pairs={{0,1},{1,0},{2,3},{3,2},{4,5},{5,4},{6,7},{7,6},{8,9},{9,8},{10,11... | collective-permute-start | bytes 798728 | tf_op jit(solution)/shard_map/ppermute | solution.py:109
  8.4 22.5 %collective-permute-start.2 = (f32[520,128]{1,0:T(8,128)}, f32[520,128]{1,0:T(8,128)S(1)}, u32[]{:S(2)}, u32[]{:S(2)}) collective-permute-start(f32[520,128]{1,0:T(8,128)} %get-tuple-element.20), channel_id=1, source_target_pairs={{0,7},{1,6},{2,5},{3,4},{4,3},{5,2},{6,1},{7,0},{8,15},{9,14},{10,... | collective-permute-start | bytes 798728 | tf_op jit(solution)/shard_map/ppermute | solution.py:109
  10.1 24.1 %collective-permute-start.3 = (f32[520,128]{1,0:T(8,128)}, f32[520,128]{1,0:T(8,128)S(1)}, u32[]{:S(2)}, u32[]{:S(2)}) collective-permute-start(f32[520,128]{1,0:T(8,128)} %get-tuple-element.20), channel_id=1, source_target_pairs={{0,3},{1,2},{2,1},{3,0},{4,7},{5,6},{6,5},{7,4},{8,11},{9,10},{10,... | collective-permute-start | bytes 798728 | tf_op jit(solution)/shard_map/ppermute | solution.py:109
  10.4 23.8 %collective-permute-start.4 = (f32[520,128]{1,0:T(8,128)}, f32[520,128]{1,0:T(8,128)S(1)}, u32[]{:S(2)}, u32[]{:S(2)}) collective-permute-start(f32[520,128]{1,0:T(8,128)} %get-tuple-element.20), channel_id=1, source_target_pairs={{0,4},{1,5},{2,6},{3,7},{4,0},{5,1},{6,2},{7,3},{8,12},{9,13},{10,... | collective-permute-start | bytes 798728 | tf_op jit(solution)/shard_map/ppermute | solution.py:109
  15.3 18.9 %collective-permute-start.5 = (f32[520,128]{1,0:T(8,128)}, f32[520,128]{1,0:T(8,128)S(1)}, u32[]{:S(2)}, u32[]{:S(2)}) collective-permute-start(f32[520,128]{1,0:T(8,128)} %get-tuple-element.20), channel_id=1, source_target_pairs={{0,2},{1,3},{2,0},{3,1},{4,6},{5,7},{6,4},{7,5},{8,10},{9,11},{10,... | collective-permute-start | bytes 798728 | tf_op jit(solution)/shard_map/ppermute | solution.py:109
  21.6 12.6 %collective-permute-start.6 = (f32[520,128]{1,0:T(8,128)}, f32[520,128]{1,0:T(8,128)S(1)}, u32[]{:S(2)}, u32[]{:S(2)}) collective-permute-start(f32[520,128]{1,0:T(8,128)} %get-tuple-element.20), channel_id=1, source_target_pairs={{0,6},{1,7},{2,4},{3,5},{4,2},{5,3},{6,0},{7,1},{8,14},{9,15},{10,... | collective-permute-start | bytes 798728 | tf_op jit(solution)/shard_map/ppermute | solution.py:109
  24.0 18.7 %all-to-all-start.1 = ((f32[8,32,512]{2,1,0:T(8,128)}), f32[8,32,512]{2,1,0:T(8,128)}, u32[]{:S(2)}, u32[]{:S(2)}) async-start(f32[8,32,512]{2,1,0:T(8,128)} %broadcast_in_dim.10), calls=%async_computation.1 | async-start | bytes 1048576 | tf_op jit(solution)/shard_map/all_to_all | solution.py:250
  38.2 4.5 %collective-permute-start.7 = (f32[8,32,512]{2,1,0:T(8,128)}, f32[8,32,512]{2,1,0:T(8,128)S(1)}, u32[]{:S(2)}, u32[]{:S(2)}) collective-permute-start(f32[8,32,512]{2,1,0:T(8,128)} %get-tuple-element.22), channel_id=1, source_target_pairs={{0,8},{8,0},{16,24},{24,16},{32,40},{40,32},{48,56},{56,48},{64,72... | collective-permute-start | bytes 1572872 | tf_op jit(solution)/shard_map/ppermute | solution.py:274
  42.7 5.5 %collective-permute-start.8 = (f32[8,32,512]{2,1,0:T(8,128)}, f32[8,32,512]{2,1,0:T(8,128)S(1)}, u32[]{:S(2)}, u32[]{:S(2)}) collective-permute-start(f32[8,32,512]{2,1,0:T(8,128)} %all-to-all-done.1.own_ref), channel_id=1, source_target_pairs={{0,8},{8,0},{16,24},{24,16},{32,40},{40,32},{48,56},{56,48},{64,72... | collective-permute-start | bytes 1572872 | tf_op jit(solution)/shard_map/ppermute | solution.py:251
  43.6 16.5 %all-to-all-start = ((f32[8,32,512]{2,1,0:T(8,128)}), f32[8,32,512]{2,1,0:T(8,128)S(1)}, u32[]{:S(2)}, u32[]{:S(2)}) async-start(f32[8,32,512]{2,1,0:T(8,128)} %pair_sum.1), calls=%async_computation | async-start | bytes 1048576 | tf_op jit(solution)/shard_map/all_to_all | solution.py:275
  60.9 12.7 %all-to-all-start.2 = ((f32[8,32,512]{2,1,0:T(8,128)}), f32[8,32,512]{2,1,0:T(8,128)S(1)}, u32[]{:S(2)}, u32[]{:S(2)}) async-start(f32[8,32,512]{2,1,0:T(8,128)} %gather_sum.1), calls=%async_computation.2 | async-start | bytes 1048576 | tf_op jit(solution)/shard_map/all_to_all | solution.py:304
  75.6 1.2 %collective-permute-start.9 = (f32[40,256]{1,0:T(8,128)S(1)}, f32[40,256]{1,0:T(8,128)S(1)}, u32[]{:S(2)}, u32[]{:S(2)}) collective-permute-start(f32[40,256]{1,0:T(8,128)S(1)} %get-tuple-element.29.a_ref), channel_id=1, source_target_pairs={{0,8},{8,0},{16,24},{24,16},{32,40},{40,32},{48,56},{56,48},{64,72... | collective-permute-start | bytes 122888 | tf_op jit(solution)/shard_map/ppermute | solution.py:323
  77.6 13.5 %all-to-all-start.3 = ((f32[8,40,256]{2,1,0:T(8,128)}), f32[8,40,256]{2,1,0:T(8,128)S(1)}, u32[]{:S(2)}, u32[]{:S(2)}) async-start(f32[8,40,256]{2,1,0:T(8,128)} %pair_grads.1), calls=%async_computation.3 | async-start | bytes 655360 | tf_op jit(solution)/shard_map/all_to_all | solution.py:324

commit v4 on v3

--- a/solution.py
+++ b/solution.py
@@ -11,9 +11,10 @@
 BF16 = jnp.bfloat16
 VMEM = pl.BlockSpec(memory_space=pltpu.VMEM)
 SMEM = pl.BlockSpec(memory_space=pltpu.SMEM)
+LIMIT = pltpu.CompilerParams(vmem_limit_bytes=16 * 2**20)
 NN = (((1,), (0,)), ((), ()))
 NT = (((1,), (1,)), ((), ()))
-TILE_ORDER = [5, 1, 7, 3, 4, 2, 6]
+TILE_ORDER = [5, 1, 4, 7, 3, 2, 6]
 
 
 def split(x):
@@ -70,7 +71,9 @@
 
 def mirror_kernel(slots, order, *refs):
     tiles_refs, refs = refs[: len(order)], refs[len(order) :]
-    x_ref, keep_ref, send_ref, side_ref, copy_ref, total, meta, meta_sems, copy_sems = refs
+    x_hbm, keep_ref, send_ref, side_ref, copy_ref, total, x_ref, meta, meta_sems, copy_sems, x_sem, send_sem = refs
+    x_copy = pltpu.make_async_copy(x_hbm, x_ref, x_sem)
+    x_copy.start()
     edge = tiles_refs[0].shape[1]
     base = slots * edge
     row_tiles = x_ref.shape[1] // edge
@@ -80,6 +83,7 @@
     total[...] = jnp.zeros_like(total)
     for d, ref in enumerate(tiles_refs):
         side_ref[d] = ref[base:, :]
+    x_copy.wait()
     for d, ref in enumerate(tiles_refs):
         metas[d].wait()
         for k in range(slots):
@@ -90,10 +94,12 @@
             lanes = pl.ds(pl.multiple_of((col % row_tiles) * edge, edge), edge)
             piece = col // row_tiles
             total[(piece % 2) ^ core, piece // 2, :, lanes] += tile_dot(x, u, NN)
+    sent = pltpu.make_async_copy(total.at[1], send_ref, send_sem)
+    sent.start()
     keep_ref[...] = total[0]
-    send_ref[...] = total[1]
     for copy in spares:
         copy.wait()
+    sent.wait()
 
 
 def add_kernel(a_ref, b_ref, out_ref):
@@ -254,15 +260,18 @@
     meta = [pltpu.SMEM((cols, 8, edge), F32), pltpu.SemaphoreType.DMA((cols,))]
     keep, send, sides, spare_tiles = pl.pallas_call(
         functools.partial(mirror_kernel, slots, order),
-        in_specs=[VMEM] * (cols + 1),
-        out_specs=[VMEM] * 3 + [anywhere],
+        in_specs=[VMEM] * cols + [anywhere],
+        out_specs=[VMEM, anywhere, VMEM, anywhere],
         out_shape=[
             pltpu.VMEM(half, F32),
-            pltpu.VMEM(half, F32),
+            jax.ShapeDtypeStruct(half, F32),
             pltpu.VMEM((cols, 8, edge), F32),
             jax.ShapeDtypeStruct((cols, length, edge), F32),
         ],
-        scratch_shapes=[pltpu.VMEM((2,) + half, F32)] + meta + [pltpu.SemaphoreType.DMA((cols,))],
+        scratch_shapes=[pltpu.VMEM((2,) + half, F32), pltpu.VMEM((block, nodes), F32)]
+        + meta
+        + [pltpu.SemaphoreType.DMA((cols,))]
+        + [pltpu.SemaphoreType.DMA] * 2,
         name="mirror",
     )(*tiles, x_own)
     paired = pl.pallas_call(
@@ -292,6 +301,7 @@
         ],
         scratch_shapes=[pltpu.VMEM((feats, edge), F32)],
         name="prep",
+        compiler_params=LIMIT,
     )(weight, on_chip(sides))
     wt, side_t, readout = on_chip(wt), on_chip(side_t), on_chip(readout)
     y_own = pl.pallas_call(
@@ -313,6 +323,7 @@
         ],
         scratch_shapes=[pltpu.VMEM((feats, ports), F32)] * 2,
         name="ports",
+        compiler_params=LIMIT,
     )(y, wt, side_t, readout, port_rows, targets)
     pair_grads = pl.pallas_call(
         add_kernel,
@@ -328,6 +339,7 @@
         out_specs=VMEM,
         out_shape=jax.ShapeDtypeStruct((block, nodes), F32),
         name="hidden",
+        compiler_params=LIMIT,
     )(y, wt, side_t)
     gw, gb, gow = pl.pallas_call(
         final_kernel,

time: 92.4 us -> 91.1 us (0.986)
  waiting for transfers between devices: 39.4 us -> 42 us
  Pallas kernels: 17.1 us -> 15 us
  starting transfers between devices: 32.1 us -> 30.4 us
    all_to_all x1, waiting for transfers between devices: 8 us -> 9.04 us  [per_device(): y = on_chip(lax.all_to_all(y_own, 'col', 0, 0))]
    ppermute x7, starting transfers between devices: 13.3 us -> 12.3 us  [xor_exchange(): return lax.ppermute(x, axis, [(i, i ^ bits) for i in range(size)])]
    pallas_call x1, Pallas kernels: 1.18 us -> 0.23 us  [per_device(): pl.pallas_call(functools.partial(prep_kernel, order), in_specs=[VMEM] * 2...]
  transfers between devices with their start and end apart: 14 -> 14, of which waited for: 8 -> 8; matrix products, arithmetic and copies ran while one was open for 2% -> 2% of each run, Pallas kernels for 12% -> 11%
where the time goes in v4:
time: 91.1 us; the launch traced here: 90.5 us
  waiting for transfers between devices  42 us (46%)
  starting transfers between devices  30.4 us (33%)
  Pallas kernels  15 us (16%)
  local copies, waits for them, and re-layouts  1.72 us (2%)
  between operations  1.37 us (2%)
    ppermute x7, starting transfers between devices, xor_exchange(): return lax.ppermute(x, axis, [(i, i ^ bits) for i in range(size)])  12.3 us
    ppermute x7, waiting for transfers between devices, xor_exchange(): return lax.ppermute(x, axis, [(i, i ^ bits) for i in range(size)])  10 us
    all_to_all x1, waiting for transfers between devices, per_device(): y = on_chip(lax.all_to_all(y_own, 'col', 0, 0))  9.04 us
    all_to_all x1, waiting for transfers between devices, per_device(): lax.all_to_all(pair_grads, 'row', 0, 0, axis_index_groups=chips)  8.9 us
    all_to_all x1, waiting for transfers between devices, per_device(): lax.all_to_all(paired, 'row', 0, 0, axis_index_groups=chips)  7.76 us
    all_to_all x1, starting transfers between devices, per_device(): own_rows = lax.all_to_all(x_copies, 'row', 0, 0, axis_index_groups=chips)  6.93 us
    all_to_all x1, waiting for transfers between devices, per_device(): own_rows = lax.all_to_all(x_copies, 'row', 0, 0, axis_index_groups=chips)  5.06 us
    pallas_call x1, Pallas kernels, per_device(): pl.pallas_call(functools.partial(direct_kernel, slots), in_specs=[VMEM] *...  4.19 us
  transfers between devices with their start and end apart: 14, of which 8 were waited for; matrix products, arithmetic and copies ran while one was open for 2% of the time, Pallas kernels for 11%

profile of v4, /device:TPU:0, one launch (start us, length us, event | category | flops | bytes accessed | tf_op | source)
XLA Modules:
  0.0 90.5 jit_solution(7113706067342063183)
XLA Ops:
  1.3 1.7 %pack.1 = (f32[520,128]{1,0:T(8,128)}, f32[520,128]{1,0:T(8,128)S(1)}) custom-call(s32[1,1,4]{2,1,0:T(1,128)} %rows_ref.1, s32[1,1,4]{2,1,0:T(1,128)} %cols_ref.1, s32[1,1]{1,0:T(1,128)S(6)} %copy.15.count_ref, f32[1,512,128]{2,1,0:T(8,128)} %bitcast.8, f32[1,32]{1,0:T(1,128)} %bitcast.10, f32[2,32]{1,0:T(2,128)} %readout_ref.1), custom_call_target="tpu_custom_call" | custom-call | tf_op jit(solution)/shard_map/pack/pallas_call | solution.py:246
  3.0 4.9 %collective-permute-start = (f32[520,128]{1,0:T(8,128)}, f32[520,128]{1,0:T(8,128)S(1)}, u32[]{:S(2)}, u32[]{:S(2)}) collective-permute-start(f32[520,128]{1,0:T(8,128)} %get-tuple-element.20), channel_id=1, source_target_pairs={{0,5},{1,4},{2,7},{3,6},{4,1},{5,0},{6,3},{7,2},{8,13},{9,12},{10,... | collective-permute-start | bytes 798728 | tf_op jit(solution)/shard_map/ppermute | solution.py:115
  8.4 4.6 %collective-permute-start.3 = (f32[520,128]{1,0:T(8,128)}, f32[520,128]{1,0:T(8,128)S(1)}, u32[]{:S(2)}, u32[]{:S(2)}) collective-permute-start(f32[520,128]{1,0:T(8,128)} %get-tuple-element.20), channel_id=1, source_target_pairs={{0,7},{1,6},{2,5},{3,4},{4,3},{5,2},{6,1},{7,0},{8,15},{9,14},{10,... | collective-permute-start | bytes 798728 | tf_op jit(solution)/shard_map/ppermute | solution.py:115
  13.0 2.3 %collective-permute-done.refs_1_ = f32[520,128]{1,0:T(8,128)S(1)} collective-permute-done((f32[520,128]{1,0:T(8,128)}, f32[520,128]{1,0:T(8,128)S(1)}, u32[]{:S(2)}, u32[]{:S(2)}) %collective-permute-start) | collective-permute-done | bytes 266272 | tf_op jit(solution)/shard_map/ppermute | solution.py:115
  15.3 1.6 %collective-permute-start.5 = (f32[520,128]{1,0:T(8,128)}, f32[520,128]{1,0:T(8,128)S(1)}, u32[]{:S(2)}, u32[]{:S(2)}) collective-permute-start(f32[520,128]{1,0:T(8,128)} %get-tuple-element.20), channel_id=1, source_target_pairs={{0,2},{1,3},{2,0},{3,1},{4,6},{5,7},{6,4},{7,5},{8,10},{9,11},{10,... | collective-permute-start | bytes 798728 | tf_op jit(solution)/shard_map/ppermute | solution.py:115
  16.9 4.7 %collective-permute-done.1.refs_2_ = f32[520,128]{1,0:T(8,128)S(1)} collective-permute-done((f32[520,128]{1,0:T(8,128)}, f32[520,128]{1,0:T(8,128)S(1)}, u32[]{:S(2)}, u32[]{:S(2)}) %collective-permute-start.1) | collective-permute-done | bytes 266272 | tf_op jit(solution)/shard_map/ppermute | solution.py:115
  22.3 1.7 %broadcast_in_dim.10 = f32[8,32,512]{2,1,0:T(8,128)} broadcast(f32[32,512]{1,0:T(8,128)} %bitcast.6), dimensions={1,2} | broadcast | bytes 589824 | tf_op jit(solution)/shard_map/broadcast_in_dim | solution.py:255
  24.0 6.9 %all-to-all-start.1 = ((f32[8,32,512]{2,1,0:T(8,128)}), f32[8,32,512]{2,1,0:T(8,128)S(1)}, u32[]{:S(2)}, u32[]{:S(2)}) async-start(f32[8,32,512]{2,1,0:T(8,128)} %broadcast_in_dim.10), calls=%async_computation.1 | async-start | bytes 1048576 | tf_op jit(solution)/shard_map/all_to_all | solution.py:256
  31.0 3.0 %collective-permute-done.4.refs_5_ = f32[520,128]{1,0:T(8,128)S(1)} collective-permute-done((f32[520,128]{1,0:T(8,128)}, f32[520,128]{1,0:T(8,128)S(1)}, u32[]{:S(2)}, u32[]{:S(2)}) %collective-permute-start.4) | collective-permute-done | bytes 266272 | tf_op jit(solution)/shard_map/ppermute | solution.py:115
  33.9 3.5 %mirror.1 = (f32[8,32,512]{2,1,0:T(8,128)S(1)}, f32[8,32,512]{2,1,0:T(8,128)}, f32[8,8,128]{2,1,0:T(8,128)S(1)}, f32[8,520,128]{2,1,0:T(8,128)}) custom-call(f32[520,128]{1,0:T(8,128)S(1)} %get-tuple-element.19.refs_0_, f32[520,128]{1,0:T(8,128)S(1)} %collective-permute-done.refs_1_, f32[520,128]{1,0:T(8,128)S(1)} %collective-permute-done.1.refs_2_, ...), custom_call_target="tpu_custom_call" | custom-call | tf_op jit(solution)/shard_map/mirror/pallas_call | solution.py:261
  37.6 5.1 %all-to-all-done.1.own_ref = f32[8,32,512]{2,1,0:T(8,128)S(1)} async-done(((f32[8,32,512]{2,1,0:T(8,128)}), f32[8,32,512]{2,1,0:T(8,128)S(1)}, u32[]{:S(2)}, u32[]{:S(2)}) %all-to-all-start.1) | async-done | bytes 524320 | tf_op jit(solution)/shard_map/all_to_all | solution.py:256
  42.6 0.9 pair_sum.1
  43.5 4.0 %all-to-all-start = ((f32[8,32,512]{2,1,0:T(8,128)}), f32[8,32,512]{2,1,0:T(8,128)S(1)}, u32[]{:S(2)}, u32[]{:S(2)}) async-start(f32[8,32,512]{2,1,0:T(8,128)} %pair_sum.1), calls=%async_computation | async-start | bytes 1048576 | tf_op jit(solution)/shard_map/all_to_all | solution.py:284
  47.5 4.2 %direct.1.direct_ref = f32[32,512]{1,0:T(8,128)S(1)} custom-call(f32[8,520,128]{2,1,0:T(8,128)} %get-tuple-element.23.tiles_ref, f32[8,32,512]{2,1,0:T(8,128)S(1)} %all-to-all-done.1.own_ref, f32[8,32,512]{2,1,0:T(8,128)S(1)} %collective-permute-done.8.other_ref), custom_call_target="tpu_custom_call" | custom-call | tf_op jit(solution)/shard_map/direct/pallas_call | solution.py:285
  51.7 7.8 %all-to-all-done.part_ref = f32[8,32,512]{2,1,0:T(8,128)S(1)} async-done(((f32[8,32,512]{2,1,0:T(8,128)}), f32[8,32,512]{2,1,0:T(8,128)S(1)}, u32[]{:S(2)}, u32[]{:S(2)}) %all-to-all-start) | async-done | bytes 524320 | tf_op jit(solution)/shard_map/all_to_all | solution.py:284
  59.5 0.9 gather_sum.1
  60.3 3.5 %all-to-all-start.2 = ((f32[8,32,512]{2,1,0:T(8,128)}), f32[8,32,512]{2,1,0:T(8,128)S(1)}, u32[]{:S(2)}, u32[]{:S(2)}) async-start(f32[8,32,512]{2,1,0:T(8,128)} %gather_sum.1), calls=%async_computation.2 | async-start | bytes 1048576 | tf_op jit(solution)/shard_map/all_to_all | solution.py:314
  64.1 9.0 %all-to-all-done.2.y_ref = f32[8,32,512]{2,1,0:T(8,128)S(1)} async-done(((f32[8,32,512]{2,1,0:T(8,128)}), f32[8,32,512]{2,1,0:T(8,128)S(1)}, u32[]{:S(2)}, u32[]{:S(2)}) %all-to-all-start.2) | async-done | bytes 524320 | tf_op jit(solution)/shard_map/all_to_all | solution.py:314
  73.1 1.3 %ports.1 = (f32[2,128]{1,0:T(2,128)}, f32[40,256]{1,0:T(8,128)S(1)}) custom-call(f32[8,32,512]{2,1,0:T(8,128)S(1)} %all-to-all-done.2.y_ref, bf16[2,256,256]{2,1,0:T(8,128)(2,1)S(1)} %get-tuple-element.25.wt_ref, f32[256,8]{1,0:T(8,128)S(1)} %get-tuple-element.26.side_t_ref, f32[8,256]{1,0:T(8,128)S(1)} %get-tuple-element.27.readout_ref, ...), custom_call_target="tpu_custom_call" | custom-call | tf_op jit(solution)/shard_map/ports/pallas_call | solution.py:316
  74.4 1.2 %collective-permute-done.9.b_ref = f32[40,256]{1,0:T(8,128)S(1)} collective-permute-done((f32[40,256]{1,0:T(8,128)S(1)}, f32[40,256]{1,0:T(8,128)S(1)}, u32[]{:S(2)}, u32[]{:S(2)}) %collective-permute-start.9) | collective-permute-done | bytes 40992 | tf_op jit(solution)/shard_map/ppermute | solution.py:334
  75.7 0.7 pair_grads.1
  76.4 3.7 %all-to-all-start.3 = ((f32[8,40,256]{2,1,0:T(8,128)}), f32[8,40,256]{2,1,0:T(8,128)S(1)}, u32[]{:S(2)}, u32[]{:S(2)}) async-start(f32[8,40,256]{2,1,0:T(8,128)} %pair_grads.1), calls=%async_computation.3 | async-start | bytes 655360 | tf_op jit(solution)/shard_map/all_to_all | solution.py:335
  80.1 0.9 hidden.1
  81.0 8.9 %all-to-all-done.3.parts_ref = f32[8,40,256]{2,1,0:T(8,128)S(1)} async-done(((f32[8,40,256]{2,1,0:T(8,128)}), f32[8,40,256]{2,1,0:T(8,128)S(1)}, u32[]{:S(2)}, u32[]{:S(2)}) %all-to-all-start.3) | async-done | bytes 327712 | tf_op jit(solution)/shard_map/all_to_all | solution.py:335
  (21 shorter events, 2.2 us)
Async XLA Ops:
  3.0 12.3 %collective-permute-start = (f32[520,128]{1,0:T(8,128)}, f32[520,128]{1,0:T(8,128)S(1)}, u32[]{:S(2)}, u32[]{:S(2)}) collective-permute-start(f32[520,128]{1,0:T(8,128)} %get-tuple-element.20), channel_id=1, source_target_pairs={{0,5},{1,4},{2,7},{3,6},{4,1},{5,0},{6,3},{7,2},{8,13},{9,12},{10,... | collective-permute-start | bytes 798728 | tf_op jit(solution)/shard_map/ppermute | solution.py:115
  7.9 13.7 %collective-permute-start.1 = (f32[520,128]{1,0:T(8,128)}, f32[520,128]{1,0:T(8,128)S(1)}, u32[]{:S(2)}, u32[]{:S(2)}) collective-permute-start(f32[520,128]{1,0:T(8,128)} %get-tuple-element.20), channel_id=1, source_target_pairs={{0,1},{1,0},{2,3},{3,2},{4,5},{5,4},{6,7},{7,6},{8,9},{9,8},{10,11... | collective-permute-start | bytes 798728 | tf_op jit(solution)/shard_map/ppermute | solution.py:115
  8.4 22.5 %collective-permute-start.2 = (f32[520,128]{1,0:T(8,128)}, f32[520,128]{1,0:T(8,128)S(1)}, u32[]{:S(2)}, u32[]{:S(2)}) collective-permute-start(f32[520,128]{1,0:T(8,128)} %get-tuple-element.20), channel_id=1, source_target_pairs={{0,4},{1,5},{2,6},{3,7},{4,0},{5,1},{6,2},{7,3},{8,12},{9,13},{10,... | collective-permute-start | bytes 798728 | tf_op jit(solution)/shard_map/ppermute | solution.py:115
  8.4 22.5 %collective-permute-start.3 = (f32[520,128]{1,0:T(8,128)}, f32[520,128]{1,0:T(8,128)S(1)}, u32[]{:S(2)}, u32[]{:S(2)}) collective-permute-start(f32[520,128]{1,0:T(8,128)} %get-tuple-element.20), channel_id=1, source_target_pairs={{0,7},{1,6},{2,5},{3,4},{4,3},{5,2},{6,1},{7,0},{8,15},{9,14},{10,... | collective-permute-start | bytes 798728 | tf_op jit(solution)/shard_map/ppermute | solution.py:115
  13.0 20.9 %collective-permute-start.4 = (f32[520,128]{1,0:T(8,128)}, f32[520,128]{1,0:T(8,128)S(1)}, u32[]{:S(2)}, u32[]{:S(2)}) collective-permute-start(f32[520,128]{1,0:T(8,128)} %get-tuple-element.20), channel_id=1, source_target_pairs={{0,3},{1,2},{2,1},{3,0},{4,7},{5,6},{6,5},{7,4},{8,11},{9,10},{10,... | collective-permute-start | bytes 798728 | tf_op jit(solution)/shard_map/ppermute | solution.py:115
  15.3 18.6 %collective-permute-start.5 = (f32[520,128]{1,0:T(8,128)}, f32[520,128]{1,0:T(8,128)S(1)}, u32[]{:S(2)}, u32[]{:S(2)}) collective-permute-start(f32[520,128]{1,0:T(8,128)} %get-tuple-element.20), channel_id=1, source_target_pairs={{0,2},{1,3},{2,0},{3,1},{4,6},{5,7},{6,4},{7,5},{8,10},{9,11},{10,... | collective-permute-start | bytes 798728 | tf_op jit(solution)/shard_map/ppermute | solution.py:115
  21.6 12.3 %collective-permute-start.6 = (f32[520,128]{1,0:T(8,128)}, f32[520,128]{1,0:T(8,128)S(1)}, u32[]{:S(2)}, u32[]{:S(2)}) collective-permute-start(f32[520,128]{1,0:T(8,128)} %get-tuple-element.20), channel_id=1, source_target_pairs={{0,6},{1,7},{2,4},{3,5},{4,2},{5,3},{6,0},{7,1},{8,14},{9,15},{10,... | collective-permute-start | bytes 798728 | tf_op jit(solution)/shard_map/ppermute | solution.py:115
  24.0 18.6 %all-to-all-start.1 = ((f32[8,32,512]{2,1,0:T(8,128)}), f32[8,32,512]{2,1,0:T(8,128)S(1)}, u32[]{:S(2)}, u32[]{:S(2)}) async-start(f32[8,32,512]{2,1,0:T(8,128)} %broadcast_in_dim.10), calls=%async_computation.1 | async-start | bytes 1048576 | tf_op jit(solution)/shard_map/all_to_all | solution.py:256
  37.5 5.2 %collective-permute-start.7 = (f32[8,32,512]{2,1,0:T(8,128)}, f32[8,32,512]{2,1,0:T(8,128)S(1)}, u32[]{:S(2)}, u32[]{:S(2)}) collective-permute-start(f32[8,32,512]{2,1,0:T(8,128)} %get-tuple-element.22), channel_id=1, source_target_pairs={{0,8},{8,0},{16,24},{24,16},{32,40},{40,32},{48,56},{56,48},{64,72... | collective-permute-start | bytes 1572872 | tf_op jit(solution)/shard_map/ppermute | solution.py:283
  42.6 4.9 %collective-permute-start.8 = (f32[8,32,512]{2,1,0:T(8,128)S(1)}, f32[8,32,512]{2,1,0:T(8,128)S(1)}, u32[]{:S(2)}, u32[]{:S(2)}) collective-permute-start(f32[8,32,512]{2,1,0:T(8,128)S(1)} %all-to-all-done.1.own_ref), channel_id=1, source_target_pairs={{0,8},{8,0},{16,24},{24,16},{32,40},{40,32},{48,56},{56,48},{64,72... | collective-permute-start | bytes 1572872 | tf_op jit(solution)/shard_map/ppermute | solution.py:257
  43.5 16.0 %all-to-all-start = ((f32[8,32,512]{2,1,0:T(8,128)}), f32[8,32,512]{2,1,0:T(8,128)S(1)}, u32[]{:S(2)}, u32[]{:S(2)}) async-start(f32[8,32,512]{2,1,0:T(8,128)} %pair_sum.1), calls=%async_computation | async-start | bytes 1048576 | tf_op jit(solution)/shard_map/all_to_all | solution.py:284
  47.5 16.4 %copy-start = (f32[256,256]{1,0:T(8,128)S(1)}, f32[256,256]{1,0:T(8,128)}, u32[]{:S(2)}) copy-start(f32[256,256]{1,0:T(8,128)} %w_ref.1) | copy-start | bytes 786436
  47.5 25.6 %copy-start.1 = (f32[2,128]{1,0:T(2,128)S(1)}, f32[2,128]{1,0:T(2,128)}, u32[]{:S(2)}) copy-start(f32[2,128]{1,0:T(2,128)} %targets_ref.1) | copy-start | bytes 3076
  47.5 25.6 %copy-start.2 = (s32[1,128]{1,0:T(1,128)S(1)}, s32[1,128]{1,0:T(1,128)}, u32[]{:S(2)}) copy-start(s32[1,128]{1,0:T(1,128)} %ports_ref.1) | copy-start | bytes 1540
  60.3 12.8 %all-to-all-start.2 = ((f32[8,32,512]{2,1,0:T(8,128)}), f32[8,32,512]{2,1,0:T(8,128)S(1)}, u32[]{:S(2)}, u32[]{:S(2)}) async-start(f32[8,32,512]{2,1,0:T(8,128)} %gather_sum.1), calls=%async_computation.2 | async-start | bytes 1048576 | tf_op jit(solution)/shard_map/all_to_all | solution.py:314
  74.4 1.2 %collective-permute-start.9 = (f32[40,256]{1,0:T(8,128)S(1)}, f32[40,256]{1,0:T(8,128)S(1)}, u32[]{:S(2)}, u32[]{:S(2)}) collective-permute-start(f32[40,256]{1,0:T(8,128)S(1)} %get-tuple-element.29.a_ref), channel_id=1, source_target_pairs={{0,8},{8,0},{16,24},{24,16},{32,40},{40,32},{48,56},{56,48},{64,72... | collective-permute-start | bytes 122888 | tf_op jit(solution)/shard_map/ppermute | solution.py:334
  76.4 13.5 %all-to-all-start.3 = ((f32[8,40,256]{2,1,0:T(8,128)}), f32[8,40,256]{2,1,0:T(8,128)S(1)}, u32[]{:S(2)}, u32[]{:S(2)}) async-start(f32[8,40,256]{2,1,0:T(8,128)} %pair_grads.1), calls=%async_computation.3 | async-start | bytes 655360 | tf_op jit(solution)/shard_map/all_to_all | solution.py:335
